TPU v7x, 32 devices: a whole 2x2x4 slice. The times are simulated.
32 devices in a mesh: grp: 2 (over x), ty: 16 (over z, y, core).
Axes of the slice: x: 2, y: 2, z: 4, core: 2. Of those that a mesh axis runs over, the one named last changes fastest.
Arguments:
- tile_object: float32 [4, 2, 4096, 768], P(None, None, ('grp', 'ty')), parts along dimension 2, may hold values from -6 to 6
- probe_wave: float32 [2, 128, 128], replicated, may hold values from -6 to 6
- propagator_phase: float32 [128, 128], replicated, may hold values from -3.140625 to 3.140625
- diffraction: float32 [128, 128, 128], P(('grp', 'ty')), parts along dimension 0, may hold values from 0 to 2
- positions: int32 [128, 2], P(('grp', 'ty')), parts along dimension 0, may hold values from 0 to 640, as said below
- counts: int32 [32], P(('grp', 'ty')), parts along dimension 0, may hold values from 0 to 4, as said below
Outputs:
- object_grad: float32 [4, 2, 4096, 768], P(None, None, ('grp', 'ty')), parts along dimension 2
There are 2 independent parts, one for each index of `grp`. A program takes and returns all parts, laid end to end along the dimension named above; an argument that names none is the same for every part. Nothing has to cross between parts.
Inputs may be any that keep to these rules, and one draw needn't show every extreme that they name: `positions`: column 0 is a row offset under 128, column 1 a column offset of at most 640. For every device d, the counts of devices 0 to d sum to between 2 * (d + 1) and 2 * (d + 2), the upper bound reached at some device; all counts sum to 32.
All inputs are finite; a program needn't handle non-finite values.
Results may differ from a plain program's by a relative error of at most 0.0003.
Values sent between devices are 32-bit elements; how exact they have to be, the bound alone decides.
A program may use at most 64 MiB of HBM per device.

v0:
```python
import jax
import jax.numpy as jnp
import numpy as np
from jax import lax
from jax.experimental import pallas as pl
from jax.experimental.pallas import tpu as pltpu
from jax.sharding import PartitionSpec as P

PS = 128
NS = 4
BF = jnp.bfloat16
F32 = jnp.float32
VMEM = pl.BlockSpec(memory_space=pltpu.VMEM)
SMEM = pl.BlockSpec(memory_space=pltpu.SMEM)


def shifted(x, axis, by):
    peers = lax.axis_size(axis)
    return lax.ppermute(x, axis, [(i, (i + by) % peers) for i in range(peers)])


def dft_parts():
    k = np.arange(PS)
    ang = (np.outer(k, k) % PS) * (2.0 * np.pi / PS)
    c = np.cos(ang) / np.sqrt(PS)
    s = -np.sin(ang) / np.sqrt(PS)
    forward = np.block([[c, s], [-s, c]]).astype(np.float32)
    inverse = np.block([[c, -s], [s, c]]).astype(np.float32)
    parts = []
    for m in (forward, inverse):
        hi = m.astype(BF)
        lo = (m - hi.astype(np.float32)).astype(BF)
        parts += [hi, lo]
    return np.stack(parts)


def crop_kernel(pos, left_ref, right_ref, out_ref):
    s = pos[pl.program_id(0), 1] % PS
    lane = lax.broadcasted_iota(jnp.int32, (PS, PS), 1)
    for a in range(NS):
        for b in range(2):
            picked = jnp.where(lane >= s, left_ref[a, b], right_ref[a, b])
            out_ref[0, a, b] = pltpu.roll(picked, (PS - s) % PS, 1)


def crop(tile, positions):
    slots = positions.shape[0]
    last = tile.shape[3] // PS - 1
    block = (NS, 2, PS, PS)
    return pl.pallas_call(
        crop_kernel,
        grid_spec=pltpu.PrefetchScalarGridSpec(
            num_scalar_prefetch=1,
            grid=(slots,),
            in_specs=[
                pl.BlockSpec(block, lambda j, pos: (0, 0, 0, pos[j, 1] // PS)),
                pl.BlockSpec(block, lambda j, pos: (0, 0, 0, jnp.minimum(pos[j, 1] // PS + 1, last))),
            ],
            out_specs=pl.BlockSpec((1,) + block, lambda j, pos: (j, 0, 0, 0, 0)),
        ),
        out_shape=jax.ShapeDtypeStruct((slots,) + block, F32),
        cost_estimate=pl.CostEstimate(flops=10**6, bytes_accessed=6 * 10**6, transcendentals=0),
    )(positions, tile, tile)


def split(x):
    hi = x.astype(BF)
    return hi, (x - hi.astype(F32)).astype(BF)


def dot(a, b):
    return jnp.dot(a, b, preferred_element_type=F32)


def stack_rows(re, im):
    return jnp.concatenate([re, im], axis=0)


def to_rows(z):
    return jnp.concatenate(
        [
            jnp.concatenate([z[:PS, :PS], z[PS:, :PS]], axis=1),
            jnp.concatenate([z[:PS, PS:], z[PS:, PS:]], axis=1),
        ],
        axis=0,
    )


def grad_kernel(pos, counts, own_ref, low_ref, probe_ref, kre_ref, kim_ref, diff_ref, tab_ref, up_ref, down_ref, t_ref, w_ref):
    pairs = range(own_ref.shape[0] // 2)
    row = lax.broadcasted_iota(jnp.int32, (PS, PS), 0)

    def left(xs, inv):
        hi, lo = tab_ref[2 - 2 * inv], tab_ref[3 - 2 * inv]
        parts = [split(x) for x in xs]
        return [dot(hi, h) + dot(hi, l) + dot(lo, h) for h, l in parts]

    def right(xs, inv):
        hi, lo = tab_ref[2 * inv], tab_ref[2 * inv + 1]
        parts = [split(x) for x in xs]
        return [dot(h, hi) + dot(l, hi) + dot(h, lo) for h, l in parts]

    def forward(xs):
        return right([to_rows(x) for x in left(xs, 0)], 0)

    def backward(xs):
        return left([to_rows(x) for x in right(xs, 1)], 1)

    for p in pairs:
        for half in range(2):
            j = 2 * p + half
            p0 = pos[j, 0]
            for a in range(NS):
                for b in range(2):
                    picked = jnp.where(row >= p0, own_ref[j, a, b], low_ref[j, a, b])
                    t_ref[a, p, b, :, half * PS : (half + 1) * PS] = pltpu.roll(picked, (PS - p0) % PS, 0)
        for b in range(2):
            w_ref[0, p, b] = jnp.concatenate([probe_ref[b]] * 2, axis=1)

    def kernel_product(z, sign):
        kre = jnp.concatenate([kre_ref[...]] * 2, axis=0)
        kim = jnp.concatenate([kim_ref[...]] * 2, axis=0) * sign
        re, im = z[:, :PS], z[:, PS:]
        return jnp.concatenate([re * kre - im * kim, re * kim + im * kre], axis=1)

    def through(s):
        xs = []
        for p in pairs:
            wre, wim, tre, tim = w_ref[s, p, 0], w_ref[s, p, 1], t_ref[s, p, 0], t_ref[s, p, 1]
            xs.append(stack_rows(wre * tre - wim * tim, wre * tim + wim * tre))
        return xs

    def advance(s, carry):
        zs = [kernel_product(z, 1.0) for z in forward(through(s))]
        for p, x in zip(pairs, backward(zs)):
            w_ref[s + 1, p, 0] = x[:PS]
            w_ref[s + 1, p, 1] = x[PS:]
        return carry

    lax.fori_loop(0, NS - 1, advance, 0)

    gs = []
    for p, z in zip(pairs, forward(through(NS - 1))):
        halves = []
        for half in range(2):
            j = 2 * p + half
            live = jnp.where(j < counts[0], 4.0, 0.0).astype(F32)
            re, im = z[half * PS : (half + 1) * PS, :PS], z[half * PS : (half + 1) * PS, PS:]
            f = (re * re + im * im - diff_ref[j]) * live
            halves.append(jnp.concatenate([re * f, im * f], axis=1))
        gs.append(jnp.concatenate(halves, axis=0))
    gs = backward(gs)

    def deposit(s, gs):
        for p in pairs:
            gre, gim = gs[p][:PS], gs[p][PS:]
            wre, wim = w_ref[s, p, 0], w_ref[s, p, 1]
            for b, val in enumerate((wre * gre + wim * gim, wre * gim - wim * gre)):
                for half in range(2):
                    j = 2 * p + half
                    p0 = pos[j, 0]
                    v = pltpu.roll(val[:, half * PS : (half + 1) * PS], p0, 0)
                    up_ref[j, s, b] = jnp.where(row >= p0, v, 0.0)
                    down_ref[j, s, b] = jnp.where(row >= p0, 0.0, v)

    def retreat(i, gs):
        s = NS - 1 - i
        deposit(s, gs)
        xs = []
        for p in pairs:
            gre, gim = gs[p][:PS], gs[p][PS:]
            tre, tim = t_ref[s, p, 0], t_ref[s, p, 1]
            xs.append(stack_rows(gre * tre + gim * tim, gim * tre - gre * tim))
        return tuple(backward([kernel_product(z, -1.0) for z in forward(xs)]))

    gs = lax.fori_loop(0, NS - 1, retreat, tuple(gs))
    deposit(0, gs)


def gradients(own, low, probe, kre, kim, diff, positions, counts):
    slots = own.shape[0]
    out = jax.ShapeDtypeStruct(own.shape, F32)
    tables = jnp.asarray(dft_parts())
    return pl.pallas_call(
        grad_kernel,
        out_shape=(out, out),
        in_specs=[SMEM, SMEM] + [VMEM] * 7,
        out_specs=(VMEM, VMEM),
        scratch_shapes=[pltpu.VMEM((NS, slots // 2, 2, PS, 2 * PS), F32)] * 2,
        compiler_params=pltpu.CompilerParams(vmem_limit_bytes=48 << 20),
        cost_estimate=pl.CostEstimate(flops=6 * 10**9, bytes_accessed=9 * 10**6, transcendentals=0),
    )(positions, counts, own, low, probe, kre, kim, diff, tables)


def place_kernel(pos, before, up_ref, down_ref, out_ref, acc_ref):
    block = pl.program_id(0)
    lane = lax.broadcasted_iota(jnp.int32, (PS, PS), 1)
    acc_ref[...] = jnp.zeros_like(acc_ref)
    for source, where in ((up_ref, pos), (down_ref, before)):
        for j in range(up_ref.shape[0]):
            k, s = where[j, 1] // PS, where[j, 1] % PS
            ours = jnp.where(k == block, 1, 0)
            bound = jnp.where(ours == 1, s, 0)
            top = jnp.where(ours == 1, PS, s)

            @pl.when((k == block) | (k + 1 == block))
            def _():
                keep = (lane >= bound) & (lane < top)
                for a in range(NS):
                    for b in range(2):
                        acc_ref[a, b] += jnp.where(keep, pltpu.roll(source[j, a, b], s, 1), 0.0)

    out_ref[...] = acc_ref[...]


def place(up, down, positions, before, width):
    block = (NS, 2, PS, PS)
    return pl.pallas_call(
        place_kernel,
        grid_spec=pltpu.PrefetchScalarGridSpec(
            num_scalar_prefetch=2,
            grid=(width // PS,),
            in_specs=[VMEM, VMEM],
            out_specs=pl.BlockSpec(block, lambda b, *_: (0, 0, 0, b)),
            scratch_shapes=[pltpu.VMEM(block, F32)],
        ),
        out_shape=jax.ShapeDtypeStruct((NS, 2, PS, width), F32),
        compiler_params=pltpu.CompilerParams(vmem_limit_bytes=32 << 20),
        cost_estimate=pl.CostEstimate(flops=10**6, bytes_accessed=7 * 10**6, transcendentals=0),
    )(positions, before, up, down)


def per_device(tile_object, probe_wave, propagator_phase, diffraction, positions, counts):
    before = shifted(positions, "ty", 1)
    low = shifted(crop(tile_object, before), "ty", -1)
    own = crop(tile_object, positions)
    kre, kim = jnp.cos(propagator_phase), jnp.sin(propagator_phase)
    up, down = gradients(own, low, probe_wave, kre, kim, diffraction, positions, counts)
    return place(up, shifted(down, "ty", 1), positions, before, tile_object.shape[3])


def solution(mesh):
    in_specs = (
        P(None, None, ("grp", "ty"), None),
        P(),
        P(),
        P(("grp", "ty"), None, None),
        P(("grp", "ty"), None),
        P(("grp", "ty")),
    )
    out_specs = P(None, None, ("grp", "ty"), None)
    return jax.shard_map(
        per_device, mesh=mesh, in_specs=in_specs, out_specs=out_specs, check_vma=False
    )
```

profile of v0, /device:TPU:0, one launch (start us, length us, event | category | flops | bytes accessed | tf_op | source)
XLA Modules:
  0.0 87.5 jit_solution(9047892508622555153)
XLA Ops:
  0.0 0.8 copy.11.pos
  0.8 0.5 collective-permute-start
  1.2 6.3 %collective-permute-done.pos.before = s32[4,2]{1,0:T(4,128)S(1)} collective-permute-done((s32[4,2]{1,0:T(4,128)S(1)}, s32[4,2]{1,0:T(4,128)S(1)}, u32[]{:S(2)}, u32[]{:S(2)}) %collective-permute-start) | collective-permute-done | bytes 64 | tf_op jit(solution)/shard_map/ppermute | solution.py:19
  7.5 0.6 copy-done.2
  8.1 5.1 %shard_map.74 = f32[4,4,2,128,128]{4,3,2,1,0:T(8,128)} custom-call(s32[4,2]{1,0:T(4,128)} %copy-done.2, f32[4,2,128,768]{3,2,1,0:T(8,128)} %right_ref.3, f32[4,2,128,768]{3,2,1,0:T(8,128)} %right_ref.3), custom_call_target="tpu_custom_call" | custom-call | flops 1000000 | bytes 6000000 | tf_op jit(solution)/shard_map/pallas_call | solution.py:50
  13.1 0.0 copy-done
  13.1 0.2 collective-permute-start.1
  14.0 0.0 copy-start.7
  14.0 0.0 copy-start.1
  14.0 0.0 copy-start.4
  14.1 0.0 copy-start.5
  14.1 0.0 copy-start.6
  14.1 5.2 %shard_map.73.own_ref = f32[4,4,2,128,128]{4,3,2,1,0:T(8,128)} custom-call(s32[4,2]{1,0:T(4,128)} %copy-done, f32[4,2,128,768]{3,2,1,0:T(8,128)} %right_ref.3, f32[4,2,128,768]{3,2,1,0:T(8,128)} %right_ref.3), custom_call_target="tpu_custom_call" | custom-call | flops 1000000 | bytes 6000000 | tf_op jit(solution)/shard_map/pallas_call | solution.py:50
  19.3 0.0 copy-done.7
  19.3 0.2 fusion
  19.5 17.7 %collective-permute-done.1.low_ref = f32[4,4,2,128,128]{4,3,2,1,0:T(8,128)S(1)} collective-permute-done((f32[4,4,2,128,128]{4,3,2,1,0:T(8,128)}, f32[4,4,2,128,128]{4,3,2,1,0:T(8,128)S(1)}, u32[]{:S(2)}, u32[]{:S(2)}) %collective-permute-start.1) | collective-permute-done | bytes 2097184 | tf_op jit(solution)/shard_map/ppermute | solution.py:19
  37.2 1.3 %copy-done.8 = f32[4,4,2,128,128]{4,3,2,1,0:T(8,128)} copy-done((f32[4,4,2,128,128]{4,3,2,1,0:T(8,128)}, f32[4,4,2,128,128]{4,3,2,1,0:T(8,128)S(1)}, u32[]{:S(2)}) %copy-start.8) | copy-done | bytes 2097176
  38.6 0.0 copy-done.1
  38.6 0.0 copy-done.4
  38.6 0.0 copy-done.5
  38.6 14.6 %shard_map.75 = (f32[4,4,2,128,128]{4,3,2,1,0:T(8,128)S(1)}, f32[4,4,2,128,128]{4,3,2,1,0:T(8,128)S(1)}) custom-call(s32[4,2]{1,0:T(4,128)S(1)} %copy-done.1, s32[1]{0:T(128)S(6)} %copy.12.counts, f32[4,4,2,128,128]{4,3,2,1,0:T(8,128)} %shard_map.73.own_ref, f32[4,4,2,128,128]{4,3,2,1,0:T(8,128)} %copy-done.8, f32[2,128,128]{2,1,0:T(8,128)S(1)} %copy-done.5, ...), custom_call_target="tpu_custom_call" | custom-call | flops 6000000000 | bytes 9000000 | tf_op jit(solution)/shard_map/pallas_call | solution.py:184
  53.2 0.1 collective-permute-start.2
  53.3 28.2 %collective-permute-done.2.down_ref = f32[4,4,2,128,128]{4,3,2,1,0:T(8,128)S(1)} collective-permute-done((f32[4,4,2,128,128]{4,3,2,1,0:T(8,128)S(1)}, f32[4,4,2,128,128]{4,3,2,1,0:T(8,128)S(1)}, u32[]{:S(2)}, u32[]{:S(2)}) %collective-permute-start.2) | collective-permute-done | bytes 2097184 | tf_op jit(solution)/shard_map/ppermute | solution.py:19
  81.5 6.0 %shard_map.76 = f32[4,2,128,768]{3,2,1,0:T(8,128)} custom-call(s32[4,2]{1,0:T(4,128)S(1)} %copy-done.1, s32[4,2]{1,0:T(4,128)S(1)} %copy-done.3, f32[4,4,2,128,128]{4,3,2,1,0:T(8,128)S(1)} %get-tuple-element.7.up_ref, f32[4,4,2,128,128]{4,3,2,1,0:T(8,128)S(1)} %collective-permute-done.2.down_ref), custom_call_target="tpu_custom_call" | custom-call | flops 1000000 | bytes 7000000 | tf_op jit(solution)/shard_map/pallas_call | solution.py:218
  (6 shorter events, 0.0 us)
Async XLA Ops:
  0.8 12.4 %copy-start = (s32[4,2]{1,0:T(4,128)}, s32[4,2]{1,0:T(4,128)S(1)}, u32[]{:S(2)}) copy-start(s32[4,2]{1,0:T(4,128)S(1)} %copy.11.pos) | copy-start | bytes 100
  0.8 6.7 %collective-permute-start = (s32[4,2]{1,0:T(4,128)S(1)}, s32[4,2]{1,0:T(4,128)S(1)}, u32[]{:S(2)}, u32[]{:S(2)}) collective-permute-start(s32[4,2]{1,0:T(4,128)S(1)} %copy.11.pos), channel_id=1, source_target_pairs={{0,1},{1,2},{2,3},{3,4},{4,5},{5,6},{6,7},{7,8},{8,9},{9,10},{10,1... | collective-permute-start | bytes 104 | tf_op jit(solution)/shard_map/ppermute | solution.py:19
  7.5 0.6 copy-start.2
  13.1 24.1 %collective-permute-start.1 = (f32[4,4,2,128,128]{4,3,2,1,0:T(8,128)}, f32[4,4,2,128,128]{4,3,2,1,0:T(8,128)S(1)}, u32[]{:S(2)}, u32[]{:S(2)}) collective-permute-start(f32[4,4,2,128,128]{4,3,2,1,0:T(8,128)} %shard_map.74), channel_id=1, source_target_pairs={{0,15},{1,0},{2,1},{3,2},{4,3},{5,4},{6,5},{7,6},{8,7},{9,8},{10,9... | collective-permute-start | bytes 6291464 | tf_op jit(solution)/shard_map/ppermute | solution.py:19
  14.0 5.3 %copy-start.7 = (f32[128,128]{1,0:T(8,128)S(1)}, f32[128,128]{1,0:T(8,128)}, u32[]{:S(2)}) copy-start(f32[128,128]{1,0:T(8,128)} %param.9) | copy-start | bytes 196612
  14.0 24.5 %copy-start.1 = (s32[4,2]{1,0:T(4,128)S(1)}, s32[4,2]{1,0:T(4,128)}, u32[]{:S(2)}) copy-start(s32[4,2]{1,0:T(4,128)} %copy-done) | copy-start | bytes 100
  14.0 24.5 %copy-start.4 = (f32[4,128,128]{2,1,0:T(8,128)S(1)}, f32[4,128,128]{2,1,0:T(8,128)}, u32[]{:S(2)}) copy-start(f32[4,128,128]{2,1,0:T(8,128)} %diff_ref.1) | copy-start | bytes 786436
  14.1 24.5 %copy-start.5 = (f32[2,128,128]{2,1,0:T(8,128)S(1)}, f32[2,128,128]{2,1,0:T(8,128)}, u32[]{:S(2)}) copy-start(f32[2,128,128]{2,1,0:T(8,128)} %probe_ref.1) | copy-start | bytes 393220
  14.1 24.5 %copy-start.6 = (bf16[4,256,256]{2,1,0:T(8,128)(2,1)S(1)}, bf16[4,256,256]{2,1,0:T(8,128)(2,1)}, u32[]{:S(2)}) copy-start(bf16[4,256,256]{2,1,0:T(8,128)(2,1)} %constant.2.clone.tab_ref) | copy-start | bytes 1572868
  37.2 1.3 %copy-start.8 = (f32[4,4,2,128,128]{4,3,2,1,0:T(8,128)}, f32[4,4,2,128,128]{4,3,2,1,0:T(8,128)S(1)}, u32[]{:S(2)}) copy-start(f32[4,4,2,128,128]{4,3,2,1,0:T(8,128)S(1)} %collective-permute-done.1.low_ref) | copy-start | bytes 6291460
  38.6 42.9 %copy-start.3 = (s32[4,2]{1,0:T(4,128)S(1)}, s32[4,2]{1,0:T(4,128)}, u32[]{:S(2)}) copy-start(s32[4,2]{1,0:T(4,128)} %copy-done.2) | copy-start | bytes 100
  53.2 28.3 %collective-permute-start.2 = (f32[4,4,2,128,128]{4,3,2,1,0:T(8,128)S(1)}, f32[4,4,2,128,128]{4,3,2,1,0:T(8,128)S(1)}, u32[]{:S(2)}, u32[]{:S(2)}) collective-permute-start(f32[4,4,2,128,128]{4,3,2,1,0:T(8,128)S(1)} %get-tuple-element.8), channel_id=1, source_target_pairs={{0,1},{1,2},{2,3},{3,4},{4,5},{5,6},{6,7},{7,8},{8,9},{9,10},{10,1... | collective-permute-start | bytes 6291464 | tf_op jit(solution)/shard_map/ppermute | solution.py:19
where the time goes:
time: 87.9 us; the launch traced here: 87.5 us
  waiting for transfers between devices  52.2 us (59%)
  Pallas kernels  30.9 us (35%)
  local copies, waits for them, and re-layouts  2.96 us (3%)
    ppermute x3, waiting for transfers between devices, shifted(): return lax.ppermute(x, axis, [(i, (i + by) % peers) for i in range(peers)])  52.2 us
    pallas_call x1, Pallas kernels, gradients(): pl.pallas_call(grad_kernel, out_shape=(out, out), in_specs=[SMEM, SMEM] +...  14.6 us
    pallas_call x2, Pallas kernels, crop(): pl.pallas_call(crop_kernel, grid_spec=pltpu.PrefetchScalarGridSpec(num_sc...  10.3 us
    pallas_call x1, Pallas kernels, place(): pl.pallas_call(place_kernel, grid_spec=pltpu.PrefetchScalarGridSpec(num_s...  6.03 us
    unnamed x19, local copies, waits for them, and re-layouts  2.72 us
  transfers between devices with their start and end apart: 3, of which 3 were waited for; matrix products, arithmetic and copies ran while one was open for 0% of the time, Pallas kernels for 6%

commit v1 on v0

--- a/solution.py
+++ b/solution.py
@@ -59,7 +59,7 @@
             out_specs=pl.BlockSpec((1,) + block, lambda j, pos: (j, 0, 0, 0, 0)),
         ),
         out_shape=jax.ShapeDtypeStruct((slots,) + block, F32),
-        cost_estimate=pl.CostEstimate(flops=10**6, bytes_accessed=6 * 10**6, transcendentals=0),
+        cost_estimate=pl.CostEstimate(flops=10**3, bytes_accessed=10**4, transcendentals=0),
     )(positions, tile, tile)
 
 
@@ -188,20 +188,25 @@
         out_specs=(VMEM, VMEM),
         scratch_shapes=[pltpu.VMEM((NS, slots // 2, 2, PS, 2 * PS), F32)] * 2,
         compiler_params=pltpu.CompilerParams(vmem_limit_bytes=48 << 20),
-        cost_estimate=pl.CostEstimate(flops=6 * 10**9, bytes_accessed=9 * 10**6, transcendentals=0),
+        cost_estimate=pl.CostEstimate(flops=3 * 10**9, bytes_accessed=5 * 10**6, transcendentals=0),
     )(positions, counts, own, low, probe, kre, kim, diff, tables)
 
 
-def place_kernel(pos, before, up_ref, down_ref, out_ref, acc_ref):
+def place_kernel(where, *refs):
+    *sources, out_ref, acc_ref = refs
     block = pl.program_id(0)
     lane = lax.broadcasted_iota(jnp.int32, (PS, PS), 1)
-    acc_ref[...] = jnp.zeros_like(acc_ref)
-    for source, where in ((up_ref, pos), (down_ref, before)):
-        for j in range(up_ref.shape[0]):
-            k, s = where[j, 1] // PS, where[j, 1] % PS
-            ours = jnp.where(k == block, 1, 0)
-            bound = jnp.where(ours == 1, s, 0)
-            top = jnp.where(ours == 1, PS, s)
+    if len(sources[0].shape) == 4:
+        acc_ref[...] = sources.pop(0)[...]
+    else:
+        acc_ref[...] = jnp.zeros_like(acc_ref)
+    row = 0
+    for source in sources:
+        for j in range(source.shape[0]):
+            k, s = where[row, 1] // PS, where[row, 1] % PS
+            row += 1
+            bound = jnp.where(k == block, s, 0)
+            top = jnp.where(k == block, PS, s)
 
             @pl.when((k == block) | (k + 1 == block))
             def _():
@@ -213,30 +218,46 @@
     out_ref[...] = acc_ref[...]
 
 
-def place(up, down, positions, before, width):
+def place(base, sources, where, width):
     block = (NS, 2, PS, PS)
+    spec = pl.BlockSpec(block, lambda b, *_: (0, 0, 0, b))
+    bases = [] if base is None else [base]
     return pl.pallas_call(
         place_kernel,
         grid_spec=pltpu.PrefetchScalarGridSpec(
-            num_scalar_prefetch=2,
+            num_scalar_prefetch=1,
             grid=(width // PS,),
-            in_specs=[VMEM, VMEM],
-            out_specs=pl.BlockSpec(block, lambda b, *_: (0, 0, 0, b)),
+            in_specs=[spec] * len(bases) + [VMEM] * len(sources),
+            out_specs=spec,
             scratch_shapes=[pltpu.VMEM(block, F32)],
         ),
         out_shape=jax.ShapeDtypeStruct((NS, 2, PS, width), F32),
         compiler_params=pltpu.CompilerParams(vmem_limit_bytes=32 << 20),
         cost_estimate=pl.CostEstimate(flops=10**6, bytes_accessed=7 * 10**6, transcendentals=0),
-    )(positions, before, up, down)
+    )(where, *bases, *sources)
 
 
 def per_device(tile_object, probe_wave, propagator_phase, diffraction, positions, counts):
+    width = tile_object.shape[3]
+    slots = positions.shape[0]
     before = shifted(positions, "ty", 1)
-    low = shifted(crop(tile_object, before), "ty", -1)
-    own = crop(tile_object, positions)
+    first, rest = slice(0, slots // 2), slice(slots // 2, slots)
+    low_a = shifted(crop(tile_object, before[first]), "ty", -1)
+    own_a, own_b = crop(tile_object, positions[first]), crop(tile_object, positions[rest])
+    where_b, own_a, own_b = lax.optimization_barrier((before[rest], own_a, own_b))
+    rest_low, _ = lax.optimization_barrier((crop(tile_object, where_b), low_a))
+    low_b = shifted(rest_low, "ty", -1)
     kre, kim = jnp.cos(propagator_phase), jnp.sin(propagator_phase)
-    up, down = gradients(own, low, probe_wave, kre, kim, diffraction, positions, counts)
-    return place(up, shifted(down, "ty", 1), positions, before, tile_object.shape[3])
+
+    def pair(own, low, part, live):
+        return gradients(own, low, probe_wave, kre, kim, diffraction[part], positions[part], live)
+
+    up_a, down_a = pair(own_a, low_a, first, counts)
+    down_a = shifted(down_a, "ty", 1)
+    up_b, down_b = pair(own_b, low_b, rest, counts - slots // 2)
+    down_b = shifted(down_b, "ty", 1)
+    base = place(None, [up_a, up_b, down_a], jnp.concatenate([positions, before[first]], axis=0), width)
+    return place(base, [down_b], before[rest], width)
 
 
 def solution(mesh):

time: 87.9 us -> 73.2 us (0.83)
  waiting for transfers between devices: 52.2 us -> 22.3 us
  Pallas kernels: 30.9 us -> 42.5 us
  starting transfers between devices: 0.75 us -> 5.12 us
    ppermute x3 -> x5, waiting for transfers between devices: 52.2 us -> 22.3 us  [shifted(): return lax.ppermute(x, axis, [(i, (i + by) % peers) for i in range(peers)])]
    pallas_call x1 -> x2, Pallas kernels: 14.6 us -> 21 us  [gradients(): pl.pallas_call(grad_kernel, out_shape=(out, out), in_specs=[SMEM, SMEM] +...]
    ppermute x3 -> x5, starting transfers between devices: 0.75 us -> 5.12 us  [shifted(): return lax.ppermute(x, axis, [(i, (i + by) % peers) for i in range(peers)])]
    pallas_call x2 -> x4, Pallas kernels: 10.3 us -> 13.3 us  [crop(): pl.pallas_call(crop_kernel, grid_spec=pltpu.PrefetchScalarGridSpec(num_sc...]
    pallas_call x1 -> x2, Pallas kernels: 6.03 us -> 8.12 us  [place(): pl.pallas_call(place_kernel, grid_spec=pltpu.PrefetchScalarGridSpec(num_s...]
    unnamed x19 -> x21, local copies, waits for them, and re-layouts: 2.72 us -> 0.81 us
    slice x0 -> x3, local copies, waits for them, and re-layouts: none -> 1.16 us  [the longest x1 0.59 us: per_device(): before[first]]
  transfers between devices with their start and end apart: 3 -> 5, of which waited for: 3 -> 5; matrix products, arithmetic and copies ran while one was open for 0% -> 1% of each run, Pallas kernels for 6% -> 48%
where the time goes in v1:
time: 73.2 us; the launch traced here: 72.9 us
  Pallas kernels  42.5 us (58%)
  waiting for transfers between devices  22.3 us (30%)
  starting transfers between devices  5.12 us (7%)
  local copies, waits for them, and re-layouts  2.21 us (3%)
  between operations  0.82 us (1%)
    ppermute x5, waiting for transfers between devices, shifted(): return lax.ppermute(x, axis, [(i, (i + by) % peers) for i in range(peers)])  22.3 us
    pallas_call x2, Pallas kernels, gradients(): pl.pallas_call(grad_kernel, out_shape=(out, out), in_specs=[SMEM, SMEM] +...  21 us
    pallas_call x4, Pallas kernels, crop(): pl.pallas_call(crop_kernel, grid_spec=pltpu.PrefetchScalarGridSpec(num_sc...  13.3 us
    pallas_call x2, Pallas kernels, place(): pl.pallas_call(place_kernel, grid_spec=pltpu.PrefetchScalarGridSpec(num_s...  8.12 us
    ppermute x5, starting transfers between devices, shifted(): return lax.ppermute(x, axis, [(i, (i + by) % peers) for i in range(peers)])  5.12 us
  transfers between devices with their start and end apart: 5, of which 5 were waited for; matrix products, arithmetic and copies ran while one was open for 1% of the time, Pallas kernels for 48%

profile of v1, /device:TPU:0, one launch (start us, length us, event | category | flops | bytes accessed | tf_op | source)
XLA Modules:
  0.0 72.9 jit_solution(5521776937799903451)
XLA Ops:
  0.0 0.8 %copy.18 = s32[4,2]{1,0:T(4,128)S(1)} copy(s32[4,2]{0,1:T(2,128)} %param.12) | data formatting | bytes 64 | tf_op args[4]
  0.8 0.5 collective-permute-start
  1.2 6.3 %collective-permute-done = s32[4,2]{1,0:T(4,128)S(1)} collective-permute-done((s32[4,2]{1,0:T(4,128)S(1)}, s32[4,2]{1,0:T(4,128)S(1)}, u32[]{:S(2)}, u32[]{:S(2)}) %collective-permute-start) | collective-permute-done | bytes 64 | tf_op jit(solution)/shard_map/ppermute | solution.py:19
  7.5 0.6 fusion.3
  8.1 3.3 %shard_map.84 = f32[2,4,2,128,128]{4,3,2,1,0:T(8,128)} custom-call(s32[2,2]{1,0:T(2,128)} %get-tuple-element.27.pos, f32[4,2,128,768]{3,2,1,0:T(8,128)} %right_ref.7, f32[4,2,128,768]{3,2,1,0:T(8,128)} %right_ref.7), custom_call_target="tpu_custom_call" | custom-call | flops 1000 | bytes 10000 | tf_op jit(solution)/shard_map/pallas_call | solution.py:50
  11.4 0.1 collective-permute-start.1
  11.4 0.6 fusion.2
  12.0 3.3 %shard_map.83.own_ref = f32[2,4,2,128,128]{4,3,2,1,0:T(8,128)} custom-call(s32[2,2]{1,0:T(2,128)} %get-tuple-element.25.pos, f32[4,2,128,768]{3,2,1,0:T(8,128)} %right_ref.7, f32[4,2,128,768]{3,2,1,0:T(8,128)} %right_ref.7), custom_call_target="tpu_custom_call" | custom-call | flops 1000 | bytes 10000 | tf_op jit(solution)/shard_map/pallas_call | solution.py:50
  15.3 3.3 %shard_map.82.own_ref = f32[2,4,2,128,128]{4,3,2,1,0:T(8,128)} custom-call(s32[2,2]{1,0:T(2,128)} %get-tuple-element.26.pos, f32[4,2,128,768]{3,2,1,0:T(8,128)} %right_ref.7, f32[4,2,128,768]{3,2,1,0:T(8,128)} %right_ref.7), custom_call_target="tpu_custom_call" | custom-call | flops 1000 | bytes 10000 | tf_op jit(solution)/shard_map/pallas_call | solution.py:50
  18.6 0.0 copy-start.5
  18.6 0.0 copy-start.6
  18.6 3.4 %shard_map.86 = f32[2,4,2,128,128]{4,3,2,1,0:T(8,128)} custom-call(s32[2,2]{1,0:T(2,128)} %get-tuple-element.16.pos.where, f32[4,2,128,768]{3,2,1,0:T(8,128)} %right_ref.7, f32[4,2,128,768]{3,2,1,0:T(8,128)} %right_ref.7), custom_call_target="tpu_custom_call" | custom-call | flops 1000 | bytes 10000 | tf_op jit(solution)/shard_map/pallas_call | solution.py:50
  22.1 2.0 %collective-permute-done.1.low_ref = f32[2,4,2,128,128]{4,3,2,1,0:T(8,128)S(1)} collective-permute-done((f32[2,4,2,128,128]{4,3,2,1,0:T(8,128)}, f32[2,4,2,128,128]{4,3,2,1,0:T(8,128)S(1)}, u32[]{:S(2)}, u32[]{:S(2)}) %collective-permute-start.1) | collective-permute-done | bytes 1048608 | tf_op jit(solution)/shard_map/ppermute | solution.py:19
  24.1 4.5 %collective-permute-start.2 = (f32[2,4,2,128,128]{4,3,2,1,0:T(8,128)}, f32[2,4,2,128,128]{4,3,2,1,0:T(8,128)S(1)}, u32[]{:S(2)}, u32[]{:S(2)}) collective-permute-start(f32[2,4,2,128,128]{4,3,2,1,0:T(8,128)} %shard_map.86), channel_id=1, source_target_pairs={{0,15},{1,0},{2,1},{3,2},{4,3},{5,4},{6,5},{7,6},{8,7},{9,8},{10,9... | collective-permute-start | bytes 3145736 | tf_op jit(solution)/shard_map/ppermute | solution.py:19
  29.2 0.2 fusion.1
  29.6 10.5 %shard_map.85 = (f32[2,4,2,128,128]{4,3,2,1,0:T(8,128)S(1)}, f32[2,4,2,128,128]{4,3,2,1,0:T(8,128)S(1)}) custom-call(s32[2,2]{1,0:T(2,128)S(1)} %copy-done.4, s32[1]{0:T(128)S(6)} %copy.22.counts, f32[2,4,2,128,128]{4,3,2,1,0:T(8,128)S(1)} %copy-done.1, f32[2,4,2,128,128]{4,3,2,1,0:T(8,128)S(1)} %collective-permute-done.1.low_ref, ...), custom_call_target="tpu_custom_call" | custom-call | flops 3000000000 | bytes 5000000 | tf_op jit(solution)/shard_map/pallas_call | solution.py:184
  40.1 0.1 collective-permute-start.3
  40.1 1.0 %collective-permute-done.2.low_ref = f32[2,4,2,128,128]{4,3,2,1,0:T(8,128)S(1)} collective-permute-done((f32[2,4,2,128,128]{4,3,2,1,0:T(8,128)}, f32[2,4,2,128,128]{4,3,2,1,0:T(8,128)S(1)}, u32[]{:S(2)}, u32[]{:S(2)}) %collective-permute-start.2) | collective-permute-done | bytes 1048608 | tf_op jit(solution)/shard_map/ppermute | solution.py:19
  41.2 10.5 %shard_map.87 = (f32[2,4,2,128,128]{4,3,2,1,0:T(8,128)S(1)}, f32[2,4,2,128,128]{4,3,2,1,0:T(8,128)S(1)}) custom-call(s32[2,2]{1,0:T(2,128)S(1)} %copy-done.3, s32[1]{0:T(128)S(6)} %sub.3.counts, f32[2,4,2,128,128]{4,3,2,1,0:T(8,128)S(1)} %copy-done, f32[2,4,2,128,128]{4,3,2,1,0:T(8,128)S(1)} %collective-permute-done.2.low_ref, f32[2,128,128]{2,1,0:T(8,128)S(1)} %copy-done.5, ...), custom_call_target="tpu_custom_call" | custom-call | flops 3000000000 | bytes 5000000 | tf_op jit(solution)/shard_map/pallas_call | solution.py:184
  51.7 0.1 collective-permute-start.4
  51.8 5.3 %collective-permute-done.3.refs_2_ = f32[2,4,2,128,128]{4,3,2,1,0:T(8,128)S(1)} collective-permute-done((f32[2,4,2,128,128]{4,3,2,1,0:T(8,128)S(1)}, f32[2,4,2,128,128]{4,3,2,1,0:T(8,128)S(1)}, u32[]{:S(2)}, u32[]{:S(2)}) %collective-permute-start.3) | collective-permute-done | bytes 1048608 | tf_op jit(solution)/shard_map/ppermute | solution.py:19
  57.1 4.1 %shard_map.88.refs_0_ = f32[4,2,128,768]{3,2,1,0:T(8,128)S(1)} custom-call(s32[6,2]{1,0:T(8,128)S(1)} %pad_add_fusion.where, f32[2,4,2,128,128]{4,3,2,1,0:T(8,128)S(1)} %get-tuple-element.14.refs_0_, f32[2,4,2,128,128]{4,3,2,1,0:T(8,128)S(1)} %get-tuple-element.18.refs_1_, f32[2,4,2,128,128]{4,3,2,1,0:T(8,128)S(1)} %collective-permute-done.3.refs_2_), custom_call_target="tpu_custom_call" | custom-call | flops 1000000 | bytes 7000000 | tf_op jit(solution)/shard_map/pallas_call | solution.py:225
  61.1 7.7 %collective-permute-done.4.refs_1_ = f32[2,4,2,128,128]{4,3,2,1,0:T(8,128)S(1)} collective-permute-done((f32[2,4,2,128,128]{4,3,2,1,0:T(8,128)S(1)}, f32[2,4,2,128,128]{4,3,2,1,0:T(8,128)S(1)}, u32[]{:S(2)}, u32[]{:S(2)}) %collective-permute-start.4) | collective-permute-done | bytes 1048608 | tf_op jit(solution)/shard_map/ppermute | solution.py:19
  68.9 4.0 %shard_map.89 = f32[4,2,128,768]{3,2,1,0:T(8,128)} custom-call(s32[2,2]{1,0:T(2,128)S(1)} %copy-done.2, f32[4,2,128,768]{3,2,1,0:T(8,128)S(1)} %shard_map.88.refs_0_, f32[2,4,2,128,128]{4,3,2,1,0:T(8,128)S(1)} %collective-permute-done.4.refs_1_), custom_call_target="tpu_custom_call" | custom-call | flops 1000000 | bytes 7000000 | tf_op jit(solution)/shard_map/pallas_call | solution.py:225
  (20 shorter events, 0.1 us)
Async XLA Ops:
  0.8 6.7 %collective-permute-start = (s32[4,2]{1,0:T(4,128)S(1)}, s32[4,2]{1,0:T(4,128)S(1)}, u32[]{:S(2)}, u32[]{:S(2)}) collective-permute-start(s32[4,2]{1,0:T(4,128)S(1)} %copy.18), channel_id=1, source_target_pairs={{0,1},{1,2},{2,3},{3,4},{4,5},{5,6},{6,7},{7,8},{8,9},{9,10},{10,1... | collective-permute-start | bytes 104 | tf_op jit(solution)/shard_map/ppermute | solution.py:19
  11.4 12.7 %collective-permute-start.1 = (f32[2,4,2,128,128]{4,3,2,1,0:T(8,128)}, f32[2,4,2,128,128]{4,3,2,1,0:T(8,128)S(1)}, u32[]{:S(2)}, u32[]{:S(2)}) collective-permute-start(f32[2,4,2,128,128]{4,3,2,1,0:T(8,128)} %shard_map.84), channel_id=1, source_target_pairs={{0,15},{1,0},{2,1},{3,2},{4,3},{5,4},{6,5},{7,6},{8,7},{9,8},{10,9... | collective-permute-start | bytes 3145736 | tf_op jit(solution)/shard_map/ppermute | solution.py:19
  18.6 10.6 %copy-start.8 = (f32[128,128]{1,0:T(8,128)S(1)}, f32[128,128]{1,0:T(8,128)}, u32[]{:S(2)}) copy-start(f32[128,128]{1,0:T(8,128)} %param.10) | copy-start | bytes 196612
  18.6 10.9 %copy-start.7 = (f32[4,128,128]{2,1,0:T(8,128)S(1)}, f32[4,128,128]{2,1,0:T(8,128)}, u32[]{:S(2)}) copy-start(f32[4,128,128]{2,1,0:T(8,128)} %param.11) | copy-start | bytes 786436
  18.6 10.9 %copy-start.1 = (f32[2,4,2,128,128]{4,3,2,1,0:T(8,128)S(1)}, f32[2,4,2,128,128]{4,3,2,1,0:T(8,128)}, u32[]{:S(2)}) copy-start(f32[2,4,2,128,128]{4,3,2,1,0:T(8,128)} %shard_map.82.own_ref) | copy-start | bytes 3145732
  18.6 10.9 %copy-start.4 = (s32[2,2]{1,0:T(2,128)S(1)}, s32[2,2]{1,0:T(2,128)}, u32[]{:S(2)}) copy-start(s32[2,2]{1,0:T(2,128)} %get-tuple-element.26.pos) | copy-start | bytes 52
  18.6 10.9 %copy-start.5 = (f32[2,128,128]{2,1,0:T(8,128)S(1)}, f32[2,128,128]{2,1,0:T(8,128)}, u32[]{:S(2)}) copy-start(f32[2,128,128]{2,1,0:T(8,128)} %probe_ref.3) | copy-start | bytes 393220
  18.6 10.9 %copy-start.6 = (bf16[4,256,256]{2,1,0:T(8,128)(2,1)S(1)}, bf16[4,256,256]{2,1,0:T(8,128)(2,1)}, u32[]{:S(2)}) copy-start(bf16[4,256,256]{2,1,0:T(8,128)(2,1)} %constant.5.clone.tab_ref) | copy-start | bytes 1572868
  24.1 17.1 %collective-permute-start.2 = (f32[2,4,2,128,128]{4,3,2,1,0:T(8,128)}, f32[2,4,2,128,128]{4,3,2,1,0:T(8,128)S(1)}, u32[]{:S(2)}, u32[]{:S(2)}) collective-permute-start(f32[2,4,2,128,128]{4,3,2,1,0:T(8,128)} %shard_map.86), channel_id=1, source_target_pairs={{0,15},{1,0},{2,1},{3,2},{4,3},{5,4},{6,5},{7,6},{8,7},{9,8},{10,9... | collective-permute-start | bytes 3145736 | tf_op jit(solution)/shard_map/ppermute | solution.py:19
  29.5 11.7 %copy-start = (f32[2,4,2,128,128]{4,3,2,1,0:T(8,128)S(1)}, f32[2,4,2,128,128]{4,3,2,1,0:T(8,128)}, u32[]{:S(2)}) copy-start(f32[2,4,2,128,128]{4,3,2,1,0:T(8,128)} %shard_map.83.own_ref) | copy-start | bytes 3145732
  29.5 11.6 %copy-start.3 = (s32[2,2]{1,0:T(2,128)S(1)}, s32[2,2]{1,0:T(2,128)}, u32[]{:S(2)}) copy-start(s32[2,2]{1,0:T(2,128)} %get-tuple-element.25.pos) | copy-start | bytes 52
  40.1 17.0 %collective-permute-start.3 = (f32[2,4,2,128,128]{4,3,2,1,0:T(8,128)S(1)}, f32[2,4,2,128,128]{4,3,2,1,0:T(8,128)S(1)}, u32[]{:S(2)}, u32[]{:S(2)}) collective-permute-start(f32[2,4,2,128,128]{4,3,2,1,0:T(8,128)S(1)} %get-tuple-element.19), channel_id=1, source_target_pairs={{0,1},{1,2},{2,3},{3,4},{4,5},{5,6},{6,7},{7,8},{8,9},{9,10},{10,1... | collective-permute-start | bytes 3145736 | tf_op jit(solution)/shard_map/ppermute | solution.py:19
  41.2 10.6 %copy-start.9 = (s32[2,2]{1,0:T(2,128)S(1)}, s32[2,2]{1,0:T(2,128)}, u32[]{:S(2)}) copy-start(s32[2,2]{1,0:T(2,128)} %get-tuple-element.27.pos) | copy-start | bytes 52
  51.7 17.1 %collective-permute-start.4 = (f32[2,4,2,128,128]{4,3,2,1,0:T(8,128)S(1)}, f32[2,4,2,128,128]{4,3,2,1,0:T(8,128)S(1)}, u32[]{:S(2)}, u32[]{:S(2)}) collective-permute-start(f32[2,4,2,128,128]{4,3,2,1,0:T(8,128)S(1)} %get-tuple-element.20), channel_id=1, source_target_pairs={{0,1},{1,2},{2,3},{3,4},{4,5},{5,6},{6,7},{7,8},{8,9},{9,10},{10,1... | collective-permute-start | bytes 3145736 | tf_op jit(solution)/shard_map/ppermute | solution.py:19
  57.1 11.8 %copy-start.2 = (s32[2,2]{1,0:T(2,128)S(1)}, s32[2,2]{1,0:T(2,128)}, u32[]{:S(2)}) copy-start(s32[2,2]{1,0:T(2,128)} %get-tuple-element.16.pos.where) | copy-start | bytes 52

commit v2 on v1

v2 whole, which is shorter than its diff:
```python
import jax
import jax.numpy as jnp
import numpy as np
from jax import lax
from jax.experimental import pallas as pl
from jax.experimental.pallas import tpu as pltpu
from jax.sharding import PartitionSpec as P

PS = 128
NS = 4
BF = jnp.bfloat16
F32 = jnp.float32
VMEM = pl.BlockSpec(memory_space=pltpu.VMEM)
SMEM = pl.BlockSpec(memory_space=pltpu.SMEM)


def shifted(x, axis, by):
    peers = lax.axis_size(axis)
    return lax.ppermute(x, axis, [(i, (i + by) % peers) for i in range(peers)])


def dft_parts():
    k = np.arange(PS)
    ang = (np.outer(k, k) % PS) * (2.0 * np.pi / PS)
    c = np.cos(ang) / np.sqrt(PS)
    s = -np.sin(ang) / np.sqrt(PS)
    forward = np.block([[c, s], [-s, c]]).astype(np.float32)
    inverse = np.block([[c, -s], [s, c]]).astype(np.float32)
    parts = []
    for m in (forward, inverse):
        hi = m.astype(BF)
        lo = (m - hi.astype(np.float32)).astype(BF)
        parts += [hi, lo]
    return np.stack(parts)


def crop_kernel(where, tile_ref, out_ref):
    last = tile_ref.shape[3] // PS - 1
    lane = lax.broadcasted_iota(jnp.int32, (PS, PS), 1)
    for j in range(out_ref.shape[0]):
        k, s = where[j, 1] // PS, where[j, 1] % PS
        here = pl.ds(pl.multiple_of(k * PS, PS), PS)
        after = pl.ds(pl.multiple_of(jnp.minimum(k + 1, last) * PS, PS), PS)
        for a in range(NS):
            for b in range(2):
                picked = jnp.where(lane >= s, tile_ref[a, b, :, here], tile_ref[a, b, :, after])
                out_ref[j, a, b] = pltpu.roll(picked, (PS - s) % PS, 1)


def crop(tile, where):
    return pl.pallas_call(
        crop_kernel,
        in_specs=[SMEM, VMEM],
        out_specs=VMEM,
        out_shape=jax.ShapeDtypeStruct((where.shape[0], NS, 2, PS, PS), F32),
        compiler_params=pltpu.CompilerParams(vmem_limit_bytes=8 << 20),
        cost_estimate=pl.CostEstimate(flops=10**3, bytes_accessed=10**4, transcendentals=0),
    )(where, tile)


def split(x):
    hi = x.astype(BF)
    return hi, (x - hi.astype(F32)).astype(BF)


def dot(a, b):
    return jnp.dot(a, b, preferred_element_type=F32)


def grad_kernel(pos, counts, own_ref, low_ref, probe_ref, kre_ref, kim_ref, diff_ref, tab_ref, up_ref, down_ref, t_ref, w_ref):
    slots = range(own_ref.shape[0])
    row = lax.broadcasted_iota(jnp.int32, (PS, PS), 0)

    def left(zs, inv):
        hi, lo = tab_ref[2 - 2 * inv], tab_ref[3 - 2 * inv]
        parts = [split(jnp.concatenate(z, axis=0)) for z in zs]
        ys = [dot(hi, h) + dot(hi, l) + dot(lo, h) for h, l in parts]
        return [(y[:PS], y[PS:]) for y in ys]

    def right(zs, inv):
        hi, lo = tab_ref[2 * inv], tab_ref[2 * inv + 1]
        parts = [split(jnp.concatenate(z, axis=1)) for z in zs]
        ys = [dot(h, hi) + dot(l, hi) + dot(h, lo) for h, l in parts]
        return [(y[:, :PS], y[:, PS:]) for y in ys]

    def forward(zs):
        return right(left(zs, 0), 0)

    def backward(zs):
        return left(right(zs, 1), 1)

    for j in slots:
        p0 = pos[j, 0]
        for a in range(NS):
            for b in range(2):
                picked = jnp.where(row >= p0, own_ref[j, a, b], low_ref[j, a, b])
                t_ref[a, j, b] = pltpu.roll(picked, (PS - p0) % PS, 0)
        for b in range(2):
            w_ref[0, j, b] = probe_ref[b]

    def kernel_product(z, sign):
        re, im = z
        kre, kim = kre_ref[...], kim_ref[...] * sign
        return re * kre - im * kim, re * kim + im * kre

    def through(s):
        zs = []
        for j in slots:
            wre, wim, tre, tim = w_ref[s, j, 0], w_ref[s, j, 1], t_ref[s, j, 0], t_ref[s, j, 1]
            zs.append((wre * tre - wim * tim, wre * tim + wim * tre))
        return zs

    def advance(s, carry):
        zs = [kernel_product(z, 1.0) for z in forward(through(s))]
        for j, z in zip(slots, backward(zs)):
            w_ref[s + 1, j, 0], w_ref[s + 1, j, 1] = z
        return carry

    lax.fori_loop(0, NS - 1, advance, 0)

    gs = []
    for j, (re, im) in zip(slots, forward(through(NS - 1))):
        live = jnp.where(j < counts[0], 4.0, 0.0).astype(F32)
        f = (re * re + im * im - diff_ref[j]) * live
        gs.append((re * f, im * f))
    gs = backward(gs)

    def deposit(s, gs):
        for j, (gre, gim) in zip(slots, gs):
            p0 = pos[j, 0]
            wre, wim = w_ref[s, j, 0], w_ref[s, j, 1]
            for b, val in enumerate((wre * gre + wim * gim, wre * gim - wim * gre)):
                v = pltpu.roll(val, p0, 0)
                up_ref[j, s, b] = jnp.where(row >= p0, v, 0.0)
                down_ref[j, s, b] = jnp.where(row >= p0, 0.0, v)

    def retreat(i, gs):
        s = NS - 1 - i
        deposit(s, gs)
        zs = []
        for j, (gre, gim) in zip(slots, gs):
            tre, tim = t_ref[s, j, 0], t_ref[s, j, 1]
            zs.append((gre * tre + gim * tim, gim * tre - gre * tim))
        return tuple(backward([kernel_product(z, -1.0) for z in forward(zs)]))

    gs = lax.fori_loop(0, NS - 1, retreat, tuple(gs))
    deposit(0, gs)


def gradients(own, low, probe, kre, kim, diff, positions, counts):
    slots = own.shape[0]
    out = jax.ShapeDtypeStruct(own.shape, F32)
    tables = jnp.asarray(dft_parts())
    return pl.pallas_call(
        grad_kernel,
        out_shape=(out, out),
        in_specs=[SMEM, SMEM] + [VMEM] * 7,
        out_specs=(VMEM, VMEM),
        scratch_shapes=[pltpu.VMEM((NS, slots, 2, PS, PS), F32)] * 2,
        compiler_params=pltpu.CompilerParams(vmem_limit_bytes=12 << 20),
        cost_estimate=pl.CostEstimate(flops=3 * 10**9, bytes_accessed=5 * 10**6, transcendentals=0),
    )(positions, counts, own, low, probe, kre, kim, diff, tables)


def place_kernel(where, *refs):
    *sources, out_ref = refs
    last = out_ref.shape[3] // PS - 1
    lane = lax.broadcasted_iota(jnp.int32, (PS, PS), 1)
    if len(sources[0].shape) == 4:
        out_ref[...] = sources.pop(0)[...]
    else:
        out_ref[...] = jnp.zeros_like(out_ref)
    row = 0
    for source in sources:
        for j in range(source.shape[0]):
            k, s = where[row, 1] // PS, where[row, 1] % PS
            row += 1
            here = pl.ds(pl.multiple_of(k * PS, PS), PS)
            after = pl.ds(pl.multiple_of(jnp.minimum(k + 1, last) * PS, PS), PS)
            for a in range(NS):
                for b in range(2):
                    moved = pltpu.roll(source[j, a, b], s, 1)
                    out_ref[a, b, :, here] += jnp.where(lane >= s, moved, 0.0)
                    out_ref[a, b, :, after] += jnp.where(lane >= s, 0.0, moved)


def place(base, sources, where, width):
    bases = [] if base is None else [base]
    return pl.pallas_call(
        place_kernel,
        in_specs=[SMEM] + [VMEM] * (len(bases) + len(sources)),
        out_specs=VMEM,
        out_shape=jax.ShapeDtypeStruct((NS, 2, PS, width), F32),
        compiler_params=pltpu.CompilerParams(vmem_limit_bytes=12 << 20),
        cost_estimate=pl.CostEstimate(flops=10**6, bytes_accessed=7 * 10**6, transcendentals=0),
    )(where, *bases, *sources)


def per_device(tile_object, probe_wave, propagator_phase, diffraction, positions, counts):
    width = tile_object.shape[3]
    slots = positions.shape[0]
    before = shifted(positions, "ty", 1)
    first, rest = slice(0, slots // 2), slice(slots // 2, slots)
    low_a = shifted(crop(tile_object, before[first]), "ty", -1)
    own_a, own_b = crop(tile_object, positions[first]), crop(tile_object, positions[rest])
    where_b, own_a, own_b = lax.optimization_barrier((before[rest], own_a, own_b))
    rest_low, _ = lax.optimization_barrier((crop(tile_object, where_b), low_a))
    low_b = shifted(rest_low, "ty", -1)
    kre, kim = jnp.cos(propagator_phase), jnp.sin(propagator_phase)

    def pair(own, low, part, live):
        return gradients(own, low, probe_wave, kre, kim, diffraction[part], positions[part], live)

    up_a, down_a = pair(own_a, low_a, first, counts)
    down_a = shifted(down_a, "ty", 1)
    up_b, down_b = pair(own_b, low_b, rest, counts - slots // 2)
    down_b = shifted(down_b, "ty", 1)
    base = place(None, [up_a, up_b, down_a], jnp.concatenate([positions, before[first]], axis=0), width)
    return place(base, [down_b], before[rest], width)


def solution(mesh):
    in_specs = (
        P(None, None, ("grp", "ty"), None),
        P(),
        P(),
        P(("grp", "ty"), None, None),
        P(("grp", "ty"), None),
        P(("grp", "ty")),
    )
    out_specs = P(None, None, ("grp", "ty"), None)
    return jax.shard_map(
        per_device, mesh=mesh, in_specs=in_specs, out_specs=out_specs, check_vma=False
    )
```

time: 73.2 us -> 68.6 us (0.937)
  Pallas kernels: 42.5 us -> 25.6 us
  waiting for transfers between devices: 22.3 us -> 32.9 us
  local copies, waits for them, and re-layouts: 2.21 us -> 3.82 us
    pallas_call x6, Pallas kernels: 21.5 us -> 8.05 us  [the longest x2 4.46 us: place(): pl.pallas_call(place_kernel, in_specs=[SMEM] + [VMEM] * (len(bases) + len...]
    ppermute x5, waiting for transfers between devices: 22.3 us -> 32.9 us  [shifted(): return lax.ppermute(x, axis, [(i, (i + by) % peers) for i in range(peers)])]
    pallas_call x2, Pallas kernels: 21 us -> 17.6 us  [gradients(): pl.pallas_call(grad_kernel, out_shape=(out, out), in_specs=[SMEM, SMEM] +...]
    unnamed x21 -> x13, local copies, waits for them, and re-layouts: 0.81 us -> 3.56 us
  transfers between devices with their start and end apart: 5 -> 5, of which waited for: 5 -> 5; matrix products, arithmetic and copies ran while one was open for 1% -> 0% of each run, Pallas kernels for 48% -> 32%
where the time goes in v2:
time: 68.6 us; the launch traced here: 68.4 us
  waiting for transfers between devices  32.9 us (48%)
  Pallas kernels  25.6 us (37%)
  starting transfers between devices  5.28 us (8%)
  local copies, waits for them, and re-layouts  3.82 us (6%)
  between operations  0.79 us (1%)
    ppermute x5, waiting for transfers between devices, shifted(): return lax.ppermute(x, axis, [(i, (i + by) % peers) for i in range(peers)])  32.9 us
    pallas_call x2, Pallas kernels, gradients(): pl.pallas_call(grad_kernel, out_shape=(out, out), in_specs=[SMEM, SMEM] +...  17.6 us
    ppermute x5, starting transfers between devices, shifted(): return lax.ppermute(x, axis, [(i, (i + by) % peers) for i in range(peers)])  5.28 us
    pallas_call x2, Pallas kernels, place(): pl.pallas_call(place_kernel, in_specs=[SMEM] + [VMEM] * (len(bases) + len...  4.46 us
    pallas_call x4, Pallas kernels, crop(): pl.pallas_call(crop_kernel, in_specs=[SMEM, VMEM], out_specs=VMEM, out_sh...  3.6 us
    unnamed x13, local copies, waits for them, and re-layouts  3.56 us
  transfers between devices with their start and end apart: 5, of which 5 were waited for; matrix products, arithmetic and copies ran while one was open for 0% of the time, Pallas kernels for 32%

profile of v2, /device:TPU:0, one launch (start us, length us, event | category | flops | bytes accessed | tf_op | source)
XLA Modules:
  0.0 68.4 jit_solution(11951524047237044864)
XLA Ops:
  0.0 0.8 %copy.18 = s32[4,2]{1,0:T(4,128)S(1)} copy(s32[4,2]{0,1:T(2,128)} %param.12) | data formatting | bytes 64 | tf_op args[4]
  0.8 0.5 collective-permute-start
  1.2 6.3 %collective-permute-done = s32[4,2]{1,0:T(4,128)S(1)} collective-permute-done((s32[4,2]{1,0:T(4,128)S(1)}, s32[4,2]{1,0:T(4,128)S(1)}, u32[]{:S(2)}, u32[]{:S(2)}) %collective-permute-start) | collective-permute-done | bytes 64 | tf_op jit(solution)/shard_map/ppermute | solution.py:19
  7.5 1.9 %copy-done = f32[4,2,128,768]{3,2,1,0:T(8,128)S(1)} copy-done((f32[4,2,128,768]{3,2,1,0:T(8,128)S(1)}, f32[4,2,128,768]{3,2,1,0:T(8,128)}, u32[]{:S(2)}) %copy-start) | copy-done | bytes 3145752
  9.4 0.9 %shard_map.84 = f32[2,4,2,128,128]{4,3,2,1,0:T(8,128)S(1)} custom-call(s32[2,2]{1,0:T(2,128)S(1)} %get-tuple-element.27.where, f32[4,2,128,768]{3,2,1,0:T(8,128)S(1)} %copy-done), custom_call_target="tpu_custom_call" | custom-call | flops 1000 | bytes 10000 | tf_op jit(solution)/shard_map/pallas_call | solution.py:51
  10.3 0.1 collective-permute-start.1
  10.4 0.9 %copy-done.1 = f32[4,2,128,768]{3,2,1,0:T(8,128)S(1)} copy-done((f32[4,2,128,768]{3,2,1,0:T(8,128)S(1)}, f32[4,2,128,768]{3,2,1,0:T(8,128)}, u32[]{:S(2)}) %copy-start.1) | copy-done | bytes 3145752
  11.3 0.9 %shard_map.83.own_ref = f32[2,4,2,128,128]{4,3,2,1,0:T(8,128)S(1)} custom-call(s32[2,2]{1,0:T(2,128)S(1)} %get-tuple-element.25.where.pos, f32[4,2,128,768]{3,2,1,0:T(8,128)S(1)} %copy-done.1), custom_call_target="tpu_custom_call" | custom-call | flops 1000 | bytes 10000 | tf_op jit(solution)/shard_map/pallas_call | solution.py:51
  12.2 0.9 %shard_map.82.own_ref = f32[2,4,2,128,128]{4,3,2,1,0:T(8,128)S(1)} custom-call(s32[2,2]{1,0:T(2,128)S(1)} %get-tuple-element.26.where.pos, f32[4,2,128,768]{3,2,1,0:T(8,128)S(1)} %copy-done.1), custom_call_target="tpu_custom_call" | custom-call | flops 1000 | bytes 10000 | tf_op jit(solution)/shard_map/pallas_call | solution.py:51
  13.1 0.0 copy-start.4
  13.1 0.0 copy-start.3
  13.1 0.9 %shard_map.86 = f32[2,4,2,128,128]{4,3,2,1,0:T(8,128)S(1)} custom-call(s32[2,2]{1,0:T(2,128)S(1)} %get-tuple-element.16.where, f32[4,2,128,768]{3,2,1,0:T(8,128)S(1)} %copy-done.1), custom_call_target="tpu_custom_call" | custom-call | flops 1000 | bytes 10000 | tf_op jit(solution)/shard_map/pallas_call | solution.py:51
  14.0 8.7 %collective-permute-done.1.low_ref = f32[2,4,2,128,128]{4,3,2,1,0:T(8,128)S(1)} collective-permute-done((f32[2,4,2,128,128]{4,3,2,1,0:T(8,128)S(1)}, f32[2,4,2,128,128]{4,3,2,1,0:T(8,128)S(1)}, u32[]{:S(2)}, u32[]{:S(2)}) %collective-permute-start.1) | collective-permute-done | bytes 1048608 | tf_op jit(solution)/shard_map/ppermute | solution.py:19
  22.7 4.6 %collective-permute-start.2 = (f32[2,4,2,128,128]{4,3,2,1,0:T(8,128)S(1)}, f32[2,4,2,128,128]{4,3,2,1,0:T(8,128)S(1)}, u32[]{:S(2)}, u32[]{:S(2)}) collective-permute-start(f32[2,4,2,128,128]{4,3,2,1,0:T(8,128)S(1)} %shard_map.86), channel_id=1, source_target_pairs={{0,15},{1,0},{2,1},{3,2},{4,3},{5,4},{6,5},{7,6},{8,7},{9,8},{10,9... | collective-permute-start | bytes 3145736 | tf_op jit(solution)/shard_map/ppermute | solution.py:19
  28.0 0.2 fusion.1
  28.3 8.8 %shard_map.85 = (f32[2,4,2,128,128]{4,3,2,1,0:T(8,128)S(1)}, f32[2,4,2,128,128]{4,3,2,1,0:T(8,128)S(1)}) custom-call(s32[2,2]{1,0:T(2,128)S(1)} %get-tuple-element.26.where.pos, s32[1]{0:T(128)S(6)} %copy.22.counts, f32[2,4,2,128,128]{4,3,2,1,0:T(8,128)S(1)} %shard_map.82.own_ref, f32[2,4,2,128,128]{4,3,2,1,0:T(8,128)S(1)} %collective-permute-done.1.low_ref, ...), custom_call_target="tpu_custom_call" | custom-call | flops 3000000000 | bytes 5000000 | tf_op jit(solution)/shard_map/pallas_call | solution.py:154
  37.1 0.1 collective-permute-start.3
  37.1 2.5 %collective-permute-done.2.low_ref = f32[2,4,2,128,128]{4,3,2,1,0:T(8,128)S(1)} collective-permute-done((f32[2,4,2,128,128]{4,3,2,1,0:T(8,128)S(1)}, f32[2,4,2,128,128]{4,3,2,1,0:T(8,128)S(1)}, u32[]{:S(2)}, u32[]{:S(2)}) %collective-permute-start.2) | collective-permute-done | bytes 1048608 | tf_op jit(solution)/shard_map/ppermute | solution.py:19
  39.6 8.8 %shard_map.87 = (f32[2,4,2,128,128]{4,3,2,1,0:T(8,128)S(1)}, f32[2,4,2,128,128]{4,3,2,1,0:T(8,128)S(1)}) custom-call(s32[2,2]{1,0:T(2,128)S(1)} %get-tuple-element.25.where.pos, s32[1]{0:T(128)S(6)} %sub.3.counts, f32[2,4,2,128,128]{4,3,2,1,0:T(8,128)S(1)} %shard_map.83.own_ref, f32[2,4,2,128,128]{4,3,2,1,0:T(8,128)S(1)} %collective-permute-done.2.low_ref, ...), custom_call_target="tpu_custom_call" | custom-call | flops 3000000000 | bytes 5000000 | tf_op jit(solution)/shard_map/pallas_call | solution.py:154
  48.4 0.1 collective-permute-start.4
  48.5 5.5 %collective-permute-done.3.refs_2_ = f32[2,4,2,128,128]{4,3,2,1,0:T(8,128)S(1)} collective-permute-done((f32[2,4,2,128,128]{4,3,2,1,0:T(8,128)S(1)}, f32[2,4,2,128,128]{4,3,2,1,0:T(8,128)S(1)}, u32[]{:S(2)}, u32[]{:S(2)}) %collective-permute-start.3) | collective-permute-done | bytes 1048608 | tf_op jit(solution)/shard_map/ppermute | solution.py:19
  54.0 1.7 %shard_map.88.refs_0_ = f32[4,2,128,768]{3,2,1,0:T(8,128)S(1)} custom-call(s32[6,2]{1,0:T(8,128)S(1)} %pad_add_fusion.where, f32[2,4,2,128,128]{4,3,2,1,0:T(8,128)S(1)} %get-tuple-element.14.refs_0_, f32[2,4,2,128,128]{4,3,2,1,0:T(8,128)S(1)} %get-tuple-element.18.refs_1_, f32[2,4,2,128,128]{4,3,2,1,0:T(8,128)S(1)} %collective-permute-done.3.refs_2_), custom_call_target="tpu_custom_call" | custom-call | flops 1000000 | bytes 7000000 | tf_op jit(solution)/shard_map/pallas_call | solution.py:189
  55.8 9.9 %collective-permute-done.4.refs_1_ = f32[2,4,2,128,128]{4,3,2,1,0:T(8,128)S(1)} collective-permute-done((f32[2,4,2,128,128]{4,3,2,1,0:T(8,128)S(1)}, f32[2,4,2,128,128]{4,3,2,1,0:T(8,128)S(1)}, u32[]{:S(2)}, u32[]{:S(2)}) %collective-permute-start.4) | collective-permute-done | bytes 1048608 | tf_op jit(solution)/shard_map/ppermute | solution.py:19
  65.7 2.7 %shard_map.89 = f32[4,2,128,768]{3,2,1,0:T(8,128)} custom-call(s32[2,2]{1,0:T(2,128)S(1)} %get-tuple-element.16.where, f32[4,2,128,768]{3,2,1,0:T(8,128)S(1)} %shard_map.88.refs_0_, f32[2,4,2,128,128]{4,3,2,1,0:T(8,128)S(1)} %collective-permute-done.4.refs_1_), custom_call_target="tpu_custom_call" | custom-call | flops 1000000 | bytes 7000000 | tf_op jit(solution)/shard_map/pallas_call | solution.py:189
  (12 shorter events, 0.1 us)
Async XLA Ops:
  0.8 6.7 %collective-permute-start = (s32[4,2]{1,0:T(4,128)S(1)}, s32[4,2]{1,0:T(4,128)S(1)}, u32[]{:S(2)}, u32[]{:S(2)}) collective-permute-start(s32[4,2]{1,0:T(4,128)S(1)} %copy.18), channel_id=1, source_target_pairs={{0,1},{1,2},{2,3},{3,4},{4,5},{5,6},{6,7},{7,8},{8,9},{9,10},{10,1... | collective-permute-start | bytes 104 | tf_op jit(solution)/shard_map/ppermute | solution.py:19
  7.5 1.9 %copy-start = (f32[4,2,128,768]{3,2,1,0:T(8,128)S(1)}, f32[4,2,128,768]{3,2,1,0:T(8,128)}, u32[]{:S(2)}) copy-start(f32[4,2,128,768]{3,2,1,0:T(8,128)} %tile_ref.7) | copy-start | bytes 9437188
  9.4 1.9 %copy-start.1 = (f32[4,2,128,768]{3,2,1,0:T(8,128)S(1)}, f32[4,2,128,768]{3,2,1,0:T(8,128)}, u32[]{:S(2)}) copy-start(f32[4,2,128,768]{3,2,1,0:T(8,128)} %tile_ref.7) | copy-start | bytes 9437188
  10.3 12.4 %collective-permute-start.1 = (f32[2,4,2,128,128]{4,3,2,1,0:T(8,128)S(1)}, f32[2,4,2,128,128]{4,3,2,1,0:T(8,128)S(1)}, u32[]{:S(2)}, u32[]{:S(2)}) collective-permute-start(f32[2,4,2,128,128]{4,3,2,1,0:T(8,128)S(1)} %shard_map.84), channel_id=1, source_target_pairs={{0,15},{1,0},{2,1},{3,2},{4,3},{5,4},{6,5},{7,6},{8,7},{9,8},{10,9... | collective-permute-start | bytes 3145736 | tf_op jit(solution)/shard_map/ppermute | solution.py:19
  13.1 14.9 %copy-start.5 = (f32[128,128]{1,0:T(8,128)S(1)}, f32[128,128]{1,0:T(8,128)}, u32[]{:S(2)}) copy-start(f32[128,128]{1,0:T(8,128)} %param.10) | copy-start | bytes 196612
  13.1 15.1 %copy-start.4 = (f32[4,128,128]{2,1,0:T(8,128)S(1)}, f32[4,128,128]{2,1,0:T(8,128)}, u32[]{:S(2)}) copy-start(f32[4,128,128]{2,1,0:T(8,128)} %param.11) | copy-start | bytes 786436
  13.1 15.2 %copy-start.2 = (f32[2,128,128]{2,1,0:T(8,128)S(1)}, f32[2,128,128]{2,1,0:T(8,128)}, u32[]{:S(2)}) copy-start(f32[2,128,128]{2,1,0:T(8,128)} %probe_ref.3) | copy-start | bytes 393220
  13.1 15.2 %copy-start.3 = (bf16[4,256,256]{2,1,0:T(8,128)(2,1)S(1)}, bf16[4,256,256]{2,1,0:T(8,128)(2,1)}, u32[]{:S(2)}) copy-start(bf16[4,256,256]{2,1,0:T(8,128)(2,1)} %constant.5.clone.tab_ref) | copy-start | bytes 1572868
  22.7 16.9 %collective-permute-start.2 = (f32[2,4,2,128,128]{4,3,2,1,0:T(8,128)S(1)}, f32[2,4,2,128,128]{4,3,2,1,0:T(8,128)S(1)}, u32[]{:S(2)}, u32[]{:S(2)}) collective-permute-start(f32[2,4,2,128,128]{4,3,2,1,0:T(8,128)S(1)} %shard_map.86), channel_id=1, source_target_pairs={{0,15},{1,0},{2,1},{3,2},{4,3},{5,4},{6,5},{7,6},{8,7},{9,8},{10,9... | collective-permute-start | bytes 3145736 | tf_op jit(solution)/shard_map/ppermute | solution.py:19
  37.1 17.0 %collective-permute-start.3 = (f32[2,4,2,128,128]{4,3,2,1,0:T(8,128)S(1)}, f32[2,4,2,128,128]{4,3,2,1,0:T(8,128)S(1)}, u32[]{:S(2)}, u32[]{:S(2)}) collective-permute-start(f32[2,4,2,128,128]{4,3,2,1,0:T(8,128)S(1)} %get-tuple-element.19), channel_id=1, source_target_pairs={{0,1},{1,2},{2,3},{3,4},{4,5},{5,6},{6,7},{7,8},{8,9},{9,10},{10,1... | collective-permute-start | bytes 3145736 | tf_op jit(solution)/shard_map/ppermute | solution.py:19
  48.4 17.2 %collective-permute-start.4 = (f32[2,4,2,128,128]{4,3,2,1,0:T(8,128)S(1)}, f32[2,4,2,128,128]{4,3,2,1,0:T(8,128)S(1)}, u32[]{:S(2)}, u32[]{:S(2)}) collective-permute-start(f32[2,4,2,128,128]{4,3,2,1,0:T(8,128)S(1)} %get-tuple-element.20), channel_id=1, source_target_pairs={{0,1},{1,2},{2,3},{3,4},{4,5},{5,6},{6,7},{7,8},{8,9},{9,10},{10,1... | collective-permute-start | bytes 3145736 | tf_op jit(solution)/shard_map/ppermute | solution.py:19

commit v3 on v2

--- a/solution.py
+++ b/solution.py
@@ -1,3 +1,5 @@
+import functools
+
 import jax
 import jax.numpy as jnp
 import numpy as np
@@ -34,11 +36,11 @@
     return np.stack(parts)
 
 
-def crop_kernel(where, tile_ref, out_ref):
+def crop_kernel(start, where, tile_ref, out_ref):
     last = tile_ref.shape[3] // PS - 1
     lane = lax.broadcasted_iota(jnp.int32, (PS, PS), 1)
     for j in range(out_ref.shape[0]):
-        k, s = where[j, 1] // PS, where[j, 1] % PS
+        k, s = where[start + j, 1] // PS, where[start + j, 1] % PS
         here = pl.ds(pl.multiple_of(k * PS, PS), PS)
         after = pl.ds(pl.multiple_of(jnp.minimum(k + 1, last) * PS, PS), PS)
         for a in range(NS):
@@ -47,12 +49,12 @@
                 out_ref[j, a, b] = pltpu.roll(picked, (PS - s) % PS, 1)
 
 
-def crop(tile, where):
-    return pl.pallas_call(
-        crop_kernel,
+def crop(tile, where, start, stop):
+    return pl.pallas_call(
+        functools.partial(crop_kernel, start),
         in_specs=[SMEM, VMEM],
         out_specs=VMEM,
-        out_shape=jax.ShapeDtypeStruct((where.shape[0], NS, 2, PS, PS), F32),
+        out_shape=jax.ShapeDtypeStruct((stop - start, NS, 2, PS, PS), F32),
         compiler_params=pltpu.CompilerParams(vmem_limit_bytes=8 << 20),
         cost_estimate=pl.CostEstimate(flops=10**3, bytes_accessed=10**4, transcendentals=0),
     )(where, tile)
@@ -67,7 +69,7 @@
     return jnp.dot(a, b, preferred_element_type=F32)
 
 
-def grad_kernel(pos, counts, own_ref, low_ref, probe_ref, kre_ref, kim_ref, diff_ref, tab_ref, up_ref, down_ref, t_ref, w_ref):
+def grad_kernel(start, pos, counts, own_ref, low_ref, probe_ref, kre_ref, kim_ref, diff_ref, tab_ref, up_ref, down_ref, t_ref, w_ref):
     slots = range(own_ref.shape[0])
     row = lax.broadcasted_iota(jnp.int32, (PS, PS), 0)
 
@@ -90,7 +92,7 @@
         return left(right(zs, 1), 1)
 
     for j in slots:
-        p0 = pos[j, 0]
+        p0 = pos[start + j, 0]
         for a in range(NS):
             for b in range(2):
                 picked = jnp.where(row >= p0, own_ref[j, a, b], low_ref[j, a, b])
@@ -120,14 +122,14 @@
 
     gs = []
     for j, (re, im) in zip(slots, forward(through(NS - 1))):
-        live = jnp.where(j < counts[0], 4.0, 0.0).astype(F32)
-        f = (re * re + im * im - diff_ref[j]) * live
+        live = jnp.where(start + j < counts[0], 4.0, 0.0).astype(F32)
+        f = (re * re + im * im - diff_ref[start + j]) * live
         gs.append((re * f, im * f))
     gs = backward(gs)
 
     def deposit(s, gs):
         for j, (gre, gim) in zip(slots, gs):
-            p0 = pos[j, 0]
+            p0 = pos[start + j, 0]
             wre, wim = w_ref[s, j, 0], w_ref[s, j, 1]
             for b, val in enumerate((wre * gre + wim * gim, wre * gim - wim * gre)):
                 v = pltpu.roll(val, p0, 0)
@@ -147,12 +149,12 @@
     deposit(0, gs)
 
 
-def gradients(own, low, probe, kre, kim, diff, positions, counts):
+def gradients(own, low, probe, kre, kim, diff, positions, counts, start):
     slots = own.shape[0]
     out = jax.ShapeDtypeStruct(own.shape, F32)
     tables = jnp.asarray(dft_parts())
     return pl.pallas_call(
-        grad_kernel,
+        functools.partial(grad_kernel, start),
         out_shape=(out, out),
         in_specs=[SMEM, SMEM] + [VMEM] * 7,
         out_specs=(VMEM, VMEM),
@@ -162,61 +164,81 @@
     )(positions, counts, own, low, probe, kre, kim, diff, tables)
 
 
-def place_kernel(where, *refs):
-    *sources, out_ref = refs
+def put(out_ref, source, j, where):
     last = out_ref.shape[3] // PS - 1
     lane = lax.broadcasted_iota(jnp.int32, (PS, PS), 1)
-    if len(sources[0].shape) == 4:
-        out_ref[...] = sources.pop(0)[...]
-    else:
-        out_ref[...] = jnp.zeros_like(out_ref)
-    row = 0
-    for source in sources:
-        for j in range(source.shape[0]):
-            k, s = where[row, 1] // PS, where[row, 1] % PS
-            row += 1
-            here = pl.ds(pl.multiple_of(k * PS, PS), PS)
-            after = pl.ds(pl.multiple_of(jnp.minimum(k + 1, last) * PS, PS), PS)
-            for a in range(NS):
-                for b in range(2):
-                    moved = pltpu.roll(source[j, a, b], s, 1)
-                    out_ref[a, b, :, here] += jnp.where(lane >= s, moved, 0.0)
-                    out_ref[a, b, :, after] += jnp.where(lane >= s, 0.0, moved)
-
-
-def place(base, sources, where, width):
-    bases = [] if base is None else [base]
-    return pl.pallas_call(
-        place_kernel,
-        in_specs=[SMEM] + [VMEM] * (len(bases) + len(sources)),
+    k, s = where[1] // PS, where[1] % PS
+    here = pl.ds(pl.multiple_of(k * PS, PS), PS)
+    after = pl.ds(pl.multiple_of(jnp.minimum(k + 1, last) * PS, PS), PS)
+    for a in range(out_ref.shape[0]):
+        for b in range(2):
+            moved = pltpu.roll(source[j, a, b], s, 1)
+            out_ref[a, b, :, here] += jnp.where(lane >= s, moved, 0.0)
+            out_ref[a, b, :, after] += jnp.where(lane >= s, 0.0, moved)
+
+
+def first_kernel(pos, before, up_a_ref, up_b_ref, down_ref, out_ref):
+    out_ref[...] = jnp.zeros_like(out_ref)
+    half = down_ref.shape[0]
+    for j in range(half):
+        put(out_ref, up_a_ref, j, (pos[j, 0], pos[j, 1]))
+        put(out_ref, up_b_ref, j, (pos[half + j, 0], pos[half + j, 1]))
+        put(out_ref, down_ref, j, (before[j, 0], before[j, 1]))
+
+
+def place_first(sources, positions, before, width):
+    return pl.pallas_call(
+        first_kernel,
+        in_specs=[SMEM] * 2 + [VMEM] * len(sources),
         out_specs=VMEM,
         out_shape=jax.ShapeDtypeStruct((NS, 2, PS, width), F32),
         compiler_params=pltpu.CompilerParams(vmem_limit_bytes=12 << 20),
         cost_estimate=pl.CostEstimate(flops=10**6, bytes_accessed=7 * 10**6, transcendentals=0),
-    )(where, *bases, *sources)
+    )(positions, before, *sources)
+
+
+def last_kernel(start, before, base_ref, down_ref, out_ref):
+    out_ref[...] = base_ref[...]
+    for j in range(down_ref.shape[0]):
+        put(out_ref, down_ref, j, (before[start + j, 0], before[start + j, 1]))
+
+
+def place_last(base, down, before, start):
+    width = base.shape[3]
+    spec = pl.BlockSpec((1, 2, PS, width), lambda a, *_: (a, 0, 0, 0))
+    return pl.pallas_call(
+        functools.partial(last_kernel, start),
+        grid_spec=pltpu.PrefetchScalarGridSpec(
+            num_scalar_prefetch=1,
+            grid=(NS,),
+            in_specs=[spec, pl.BlockSpec((down.shape[0], 1, 2, PS, PS), lambda a, *_: (0, a, 0, 0, 0))],
+            out_specs=spec,
+        ),
+        out_shape=jax.ShapeDtypeStruct(base.shape, F32),
+        compiler_params=pltpu.CompilerParams(vmem_limit_bytes=12 << 20),
+        cost_estimate=pl.CostEstimate(flops=10**6, bytes_accessed=7 * 10**6, transcendentals=0),
+    )(before, base, down)
 
 
 def per_device(tile_object, probe_wave, propagator_phase, diffraction, positions, counts):
     width = tile_object.shape[3]
     slots = positions.shape[0]
+    half = slots // 2
     before = shifted(positions, "ty", 1)
-    first, rest = slice(0, slots // 2), slice(slots // 2, slots)
-    low_a = shifted(crop(tile_object, before[first]), "ty", -1)
-    own_a, own_b = crop(tile_object, positions[first]), crop(tile_object, positions[rest])
-    where_b, own_a, own_b = lax.optimization_barrier((before[rest], own_a, own_b))
-    rest_low, _ = lax.optimization_barrier((crop(tile_object, where_b), low_a))
-    low_b = shifted(rest_low, "ty", -1)
+    low_a = shifted(crop(tile_object, before, 0, half), "ty", -1)
     kre, kim = jnp.cos(propagator_phase), jnp.sin(propagator_phase)
-
-    def pair(own, low, part, live):
-        return gradients(own, low, probe_wave, kre, kim, diffraction[part], positions[part], live)
-
-    up_a, down_a = pair(own_a, low_a, first, counts)
+    low_b = shifted(crop(tile_object, before, half, slots), "ty", -1)
+    own_a, own_b = crop(tile_object, positions, 0, half), crop(tile_object, positions, half, slots)
+
+    def pair(own, low, start):
+        return gradients(own, low, probe_wave, kre, kim, diffraction, positions, counts, start)
+
+    up_a, down_a = pair(own_a, low_a, 0)
     down_a = shifted(down_a, "ty", 1)
-    up_b, down_b = pair(own_b, low_b, rest, counts - slots // 2)
+    up_b, down_b = pair(own_b, low_b, half)
     down_b = shifted(down_b, "ty", 1)
-    base = place(None, [up_a, up_b, down_a], jnp.concatenate([positions, before[first]], axis=0), width)
-    return place(base, [down_b], before[rest], width)
+    base = place_first([up_a, up_b, down_a], positions, before, width)
+    return place_last(base, down_b, before, half)
 
 
 def solution(mesh):

time: 68.6 us -> 63.2 us (0.921)
  waiting for transfers between devices: 32.9 us -> 30.2 us
  starting transfers between devices: 5.28 us -> 3.09 us
  local copies, waits for them, and re-layouts: 3.82 us -> 2.92 us
    ppermute x5, waiting for transfers between devices: 32.9 us -> 30.2 us  [shifted(): return lax.ppermute(x, axis, [(i, (i + by) % peers) for i in range(peers)])]
    ppermute x5, starting transfers between devices: 5.28 us -> 3.09 us  [shifted(): return lax.ppermute(x, axis, [(i, (i + by) % peers) for i in range(peers)])]
    unnamed x13, local copies, waits for them, and re-layouts: 3.56 us -> 2.68 us
  transfers between devices with their start and end apart: 5 -> 5, of which waited for: 5 -> 5; matrix products, arithmetic and copies ran while one was open for 0% -> 0% of each run, Pallas kernels for 32% -> 35%
where the time goes in v3:
time: 63.2 us; the launch traced here: 63.1 us
  waiting for transfers between devices  30.2 us (48%)
  Pallas kernels  26.1 us (41%)
  starting transfers between devices  3.09 us (5%)
  local copies, waits for them, and re-layouts  2.92 us (5%)
  between operations  0.76 us (1%)
    ppermute x5, waiting for transfers between devices, shifted(): return lax.ppermute(x, axis, [(i, (i + by) % peers) for i in range(peers)])  30.2 us
    pallas_call x2, Pallas kernels, gradients(): pl.pallas_call(functools.partial(grad_kernel, start), out_shape=(out, out...  17.7 us
    pallas_call x4, Pallas kernels, crop(): pl.pallas_call(functools.partial(crop_kernel, start), in_specs=[SMEM, VME...  3.65 us
    ppermute x5, starting transfers between devices, shifted(): return lax.ppermute(x, axis, [(i, (i + by) % peers) for i in range(peers)])  3.09 us
    pallas_call x1, Pallas kernels, place_last(): pl.pallas_call(functools.partial(last_kernel, start), grid_spec=pltpu.Pre...  2.99 us
    unnamed x13, local copies, waits for them, and re-layouts  2.68 us
    pallas_call x1, Pallas kernels, place_first(): pl.pallas_call(first_kernel, in_specs=[SMEM] * 2 + [VMEM] * len(sources),...  1.74 us
  transfers between devices with their start and end apart: 5, of which 5 were waited for; matrix products, arithmetic and copies ran while one was open for 0% of the time, Pallas kernels for 35%

profile of v3, /device:TPU:0, one launch (start us, length us, event | category | flops | bytes accessed | tf_op | source)
XLA Modules:
  0.0 63.1 jit_solution(15436308713412102358)
XLA Ops:
  0.0 0.8 %copy.9.where.pos = s32[4,2]{1,0:T(4,128)S(1)} copy(s32[4,2]{0,1:T(2,128)} %param.12) | data formatting | bytes 64 | tf_op args[4]
  0.8 0.5 collective-permute-start
  1.2 6.3 %collective-permute-done.where.before = s32[4,2]{1,0:T(4,128)S(1)} collective-permute-done((s32[4,2]{1,0:T(4,128)S(1)}, s32[4,2]{1,0:T(4,128)S(1)}, u32[]{:S(2)}, u32[]{:S(2)}) %collective-permute-start) | collective-permute-done | bytes 64 | tf_op jit(solution)/shard_map/ppermute | solution.py:21
  7.5 1.9 %copy-done = f32[4,2,128,768]{3,2,1,0:T(8,128)S(1)} copy-done((f32[4,2,128,768]{3,2,1,0:T(8,128)S(1)}, f32[4,2,128,768]{3,2,1,0:T(8,128)}, u32[]{:S(2)}) %copy-start) | copy-done | bytes 3145752
  9.4 0.9 %shard_map.83 = f32[2,4,2,128,128]{4,3,2,1,0:T(8,128)S(1)} custom-call(s32[4,2]{1,0:T(4,128)S(1)} %collective-permute-done.where.before, f32[4,2,128,768]{3,2,1,0:T(8,128)S(1)} %copy-done), custom_call_target="tpu_custom_call" | custom-call | flops 1000 | bytes 10000 | tf_op jit(solution)/shard_map/pallas_call | solution.py:53
  10.3 0.1 collective-permute-start.1
  10.4 0.9 %shard_map.86 = f32[2,4,2,128,128]{4,3,2,1,0:T(8,128)S(1)} custom-call(s32[4,2]{1,0:T(4,128)S(1)} %collective-permute-done.where.before, f32[4,2,128,768]{3,2,1,0:T(8,128)S(1)} %copy-done), custom_call_target="tpu_custom_call" | custom-call | flops 1000 | bytes 10000 | tf_op jit(solution)/shard_map/pallas_call | solution.py:53
  11.3 2.4 %collective-permute-start.2 = (f32[2,4,2,128,128]{4,3,2,1,0:T(8,128)S(1)}, f32[2,4,2,128,128]{4,3,2,1,0:T(8,128)S(1)}, u32[]{:S(2)}, u32[]{:S(2)}) collective-permute-start(f32[2,4,2,128,128]{4,3,2,1,0:T(8,128)S(1)} %shard_map.86), channel_id=1, source_target_pairs={{0,15},{1,0},{2,1},{3,2},{4,3},{5,4},{6,5},{7,6},{8,7},{9,8},{10,9... | collective-permute-start | bytes 3145736 | tf_op jit(solution)/shard_map/ppermute | solution.py:21
  13.7 0.9 %shard_map.85.own_ref = f32[2,4,2,128,128]{4,3,2,1,0:T(8,128)S(1)} custom-call(s32[4,2]{1,0:T(4,128)S(1)} %copy.9.where.pos, f32[4,2,128,768]{3,2,1,0:T(8,128)S(1)} %copy-done.1), custom_call_target="tpu_custom_call" | custom-call | flops 1000 | bytes 10000 | tf_op jit(solution)/shard_map/pallas_call | solution.py:53
  14.7 0.0 copy-start.2
  14.7 0.0 copy-start.3
  14.7 0.0 copy-start.4
  14.7 0.9 %shard_map.82.own_ref = f32[2,4,2,128,128]{4,3,2,1,0:T(8,128)S(1)} custom-call(s32[4,2]{1,0:T(4,128)S(1)} %copy.9.where.pos, f32[4,2,128,768]{3,2,1,0:T(8,128)S(1)} %copy-done.1), custom_call_target="tpu_custom_call" | custom-call | flops 1000 | bytes 10000 | tf_op jit(solution)/shard_map/pallas_call | solution.py:53
  16.3 0.2 fusion
  16.5 6.2 %collective-permute-done.1.low_ref = f32[2,4,2,128,128]{4,3,2,1,0:T(8,128)S(1)} collective-permute-done((f32[2,4,2,128,128]{4,3,2,1,0:T(8,128)S(1)}, f32[2,4,2,128,128]{4,3,2,1,0:T(8,128)S(1)}, u32[]{:S(2)}, u32[]{:S(2)}) %collective-permute-start.1) | collective-permute-done | bytes 1048608 | tf_op jit(solution)/shard_map/ppermute | solution.py:21
  22.7 8.9 %shard_map.84 = (f32[2,4,2,128,128]{4,3,2,1,0:T(8,128)S(1)}, f32[2,4,2,128,128]{4,3,2,1,0:T(8,128)S(1)}) custom-call(s32[4,2]{1,0:T(4,128)S(1)} %copy.9.where.pos, s32[1]{0:T(128)S(6)} %copy.15.counts, f32[2,4,2,128,128]{4,3,2,1,0:T(8,128)S(1)} %shard_map.82.own_ref, f32[2,4,2,128,128]{4,3,2,1,0:T(8,128)S(1)} %collective-permute-done.1.low_ref, ...), custom_call_target="tpu_custom_call" | custom-call | flops 3000000000 | bytes 5000000 | tf_op jit(solution)/shard_map/pallas_call | solution.py:156
  31.6 0.1 collective-permute-start.3
  31.7 2.3 %collective-permute-done.2.low_ref = f32[2,4,2,128,128]{4,3,2,1,0:T(8,128)S(1)} collective-permute-done((f32[2,4,2,128,128]{4,3,2,1,0:T(8,128)S(1)}, f32[2,4,2,128,128]{4,3,2,1,0:T(8,128)S(1)}, u32[]{:S(2)}, u32[]{:S(2)}) %collective-permute-start.2) | collective-permute-done | bytes 1048608 | tf_op jit(solution)/shard_map/ppermute | solution.py:21
  34.0 8.9 %shard_map.87 = (f32[2,4,2,128,128]{4,3,2,1,0:T(8,128)S(1)}, f32[2,4,2,128,128]{4,3,2,1,0:T(8,128)S(1)}) custom-call(s32[4,2]{1,0:T(4,128)S(1)} %copy.9.where.pos, s32[1]{0:T(128)S(6)} %copy.15.counts, f32[2,4,2,128,128]{4,3,2,1,0:T(8,128)S(1)} %shard_map.85.own_ref, f32[2,4,2,128,128]{4,3,2,1,0:T(8,128)S(1)} %collective-permute-done.2.low_ref, ...), custom_call_target="tpu_custom_call" | custom-call | flops 3000000000 | bytes 5000000 | tf_op jit(solution)/shard_map/pallas_call | solution.py:156
  42.8 0.1 collective-permute-start.4
  42.9 5.8 %collective-permute-done.3.down_ref = f32[2,4,2,128,128]{4,3,2,1,0:T(8,128)S(1)} collective-permute-done((f32[2,4,2,128,128]{4,3,2,1,0:T(8,128)S(1)}, f32[2,4,2,128,128]{4,3,2,1,0:T(8,128)S(1)}, u32[]{:S(2)}, u32[]{:S(2)}) %collective-permute-start.3) | collective-permute-done | bytes 1048608 | tf_op jit(solution)/shard_map/ppermute | solution.py:21
  48.7 1.7 %shard_map.88.base_ref = f32[4,2,128,768]{3,2,1,0:T(8,128)S(1)} custom-call(s32[4,2]{1,0:T(4,128)S(1)} %copy.9.where.pos, s32[4,2]{1,0:T(4,128)S(1)} %collective-permute-done.where.before, f32[2,4,2,128,128]{4,3,2,1,0:T(8,128)S(1)} %get-tuple-element.9.up_a_ref, f32[2,4,2,128,128]{4,3,2,1,0:T(8,128)S(1)} %get-tuple-element.10.up_b_ref, ...), custom_call_target="tpu_custom_call" | custom-call | flops 1000000 | bytes 7000000 | tf_op jit(solution)/shard_map/pallas_call | solution.py:190
  50.5 9.6 %collective-permute-done.4.down_ref = f32[2,4,2,128,128]{4,3,2,1,0:T(8,128)S(1)} collective-permute-done((f32[2,4,2,128,128]{4,3,2,1,0:T(8,128)S(1)}, f32[2,4,2,128,128]{4,3,2,1,0:T(8,128)S(1)}, u32[]{:S(2)}, u32[]{:S(2)}) %collective-permute-start.4) | collective-permute-done | bytes 1048608 | tf_op jit(solution)/shard_map/ppermute | solution.py:21
  60.1 3.0 %shard_map.89 = f32[4,2,128,768]{3,2,1,0:T(8,128)} custom-call(s32[4,2]{1,0:T(4,128)S(1)} %collective-permute-done.where.before, f32[4,2,128,768]{3,2,1,0:T(8,128)S(1)} %shard_map.88.base_ref, f32[2,4,2,128,128]{4,3,2,1,0:T(8,128)S(1)} %collective-permute-done.4.down_ref), custom_call_target="tpu_custom_call" | custom-call | flops 1000000 | bytes 7000000 | tf_op jit(solution)/shard_map/pallas_call | solution.py:209
  (8 shorter events, 0.0 us)
Async XLA Ops:
  0.8 6.7 %collective-permute-start = (s32[4,2]{1,0:T(4,128)S(1)}, s32[4,2]{1,0:T(4,128)S(1)}, u32[]{:S(2)}, u32[]{:S(2)}) collective-permute-start(s32[4,2]{1,0:T(4,128)S(1)} %copy.9.where.pos), channel_id=1, source_target_pairs={{0,1},{1,2},{2,3},{3,4},{4,5},{5,6},{6,7},{7,8},{8,9},{9,10},{10,1... | collective-permute-start | bytes 104 | tf_op jit(solution)/shard_map/ppermute | solution.py:21
  7.5 1.9 %copy-start = (f32[4,2,128,768]{3,2,1,0:T(8,128)S(1)}, f32[4,2,128,768]{3,2,1,0:T(8,128)}, u32[]{:S(2)}) copy-start(f32[4,2,128,768]{3,2,1,0:T(8,128)} %tile_ref.7) | copy-start | bytes 9437188
  10.3 3.4 %copy-start.1 = (f32[4,2,128,768]{3,2,1,0:T(8,128)S(1)}, f32[4,2,128,768]{3,2,1,0:T(8,128)}, u32[]{:S(2)}) copy-start(f32[4,2,128,768]{3,2,1,0:T(8,128)} %tile_ref.7) | copy-start | bytes 9437188
  10.3 12.4 %collective-permute-start.1 = (f32[2,4,2,128,128]{4,3,2,1,0:T(8,128)S(1)}, f32[2,4,2,128,128]{4,3,2,1,0:T(8,128)S(1)}, u32[]{:S(2)}, u32[]{:S(2)}) collective-permute-start(f32[2,4,2,128,128]{4,3,2,1,0:T(8,128)S(1)} %shard_map.83), channel_id=1, source_target_pairs={{0,15},{1,0},{2,1},{3,2},{4,3},{5,4},{6,5},{7,6},{8,7},{9,8},{10,9... | collective-permute-start | bytes 3145736 | tf_op jit(solution)/shard_map/ppermute | solution.py:21
  11.3 22.6 %collective-permute-start.2 = (f32[2,4,2,128,128]{4,3,2,1,0:T(8,128)S(1)}, f32[2,4,2,128,128]{4,3,2,1,0:T(8,128)S(1)}, u32[]{:S(2)}, u32[]{:S(2)}) collective-permute-start(f32[2,4,2,128,128]{4,3,2,1,0:T(8,128)S(1)} %shard_map.86), channel_id=1, source_target_pairs={{0,15},{1,0},{2,1},{3,2},{4,3},{5,4},{6,5},{7,6},{8,7},{9,8},{10,9... | collective-permute-start | bytes 3145736 | tf_op jit(solution)/shard_map/ppermute | solution.py:21
  14.6 1.6 %copy-start.5 = (f32[128,128]{1,0:T(8,128)S(1)}, f32[128,128]{1,0:T(8,128)}, u32[]{:S(2)}) copy-start(f32[128,128]{1,0:T(8,128)} %param.10) | copy-start | bytes 196612
  14.7 8.1 %copy-start.2 = (f32[4,128,128]{2,1,0:T(8,128)S(1)}, f32[4,128,128]{2,1,0:T(8,128)}, u32[]{:S(2)}) copy-start(f32[4,128,128]{2,1,0:T(8,128)} %diff_ref.3) | copy-start | bytes 786436
  14.7 8.1 %copy-start.3 = (f32[2,128,128]{2,1,0:T(8,128)S(1)}, f32[2,128,128]{2,1,0:T(8,128)}, u32[]{:S(2)}) copy-start(f32[2,128,128]{2,1,0:T(8,128)} %probe_ref.3) | copy-start | bytes 393220
  14.7 8.0 %copy-start.4 = (bf16[4,256,256]{2,1,0:T(8,128)(2,1)S(1)}, bf16[4,256,256]{2,1,0:T(8,128)(2,1)}, u32[]{:S(2)}) copy-start(bf16[4,256,256]{2,1,0:T(8,128)(2,1)} %constant.2.clone.tab_ref) | copy-start | bytes 1572868
  31.6 17.1 %collective-permute-start.3 = (f32[2,4,2,128,128]{4,3,2,1,0:T(8,128)S(1)}, f32[2,4,2,128,128]{4,3,2,1,0:T(8,128)S(1)}, u32[]{:S(2)}, u32[]{:S(2)}) collective-permute-start(f32[2,4,2,128,128]{4,3,2,1,0:T(8,128)S(1)} %get-tuple-element.11), channel_id=1, source_target_pairs={{0,1},{1,2},{2,3},{3,4},{4,5},{5,6},{6,7},{7,8},{8,9},{9,10},{10,1... | collective-permute-start | bytes 3145736 | tf_op jit(solution)/shard_map/ppermute | solution.py:21
  42.8 17.2 %collective-permute-start.4 = (f32[2,4,2,128,128]{4,3,2,1,0:T(8,128)S(1)}, f32[2,4,2,128,128]{4,3,2,1,0:T(8,128)S(1)}, u32[]{:S(2)}, u32[]{:S(2)}) collective-permute-start(f32[2,4,2,128,128]{4,3,2,1,0:T(8,128)S(1)} %get-tuple-element.12), channel_id=1, source_target_pairs={{0,1},{1,2},{2,3},{3,4},{4,5},{5,6},{6,7},{7,8},{8,9},{9,10},{10,1... | collective-permute-start | bytes 3145736 | tf_op jit(solution)/shard_map/ppermute | solution.py:21

commit v4 on v3

--- a/solution.py
+++ b/solution.py
@@ -70,7 +70,7 @@
 
 
 def grad_kernel(start, pos, counts, own_ref, low_ref, probe_ref, kre_ref, kim_ref, diff_ref, tab_ref, up_ref, down_ref, t_ref, w_ref):
-    slots = range(own_ref.shape[0])
+    slots = range(low_ref.shape[0])
     row = lax.broadcasted_iota(jnp.int32, (PS, PS), 0)
 
     def left(zs, inv):
@@ -95,7 +95,7 @@
         p0 = pos[start + j, 0]
         for a in range(NS):
             for b in range(2):
-                picked = jnp.where(row >= p0, own_ref[j, a, b], low_ref[j, a, b])
+                picked = jnp.where(row >= p0, own_ref[start + j, a, b], low_ref[j, a, b])
                 t_ref[a, j, b] = pltpu.roll(picked, (PS - p0) % PS, 0)
         for b in range(2):
             w_ref[0, j, b] = probe_ref[b]
@@ -150,8 +150,8 @@
 
 
 def gradients(own, low, probe, kre, kim, diff, positions, counts, start):
-    slots = own.shape[0]
-    out = jax.ShapeDtypeStruct(own.shape, F32)
+    slots = low.shape[0]
+    out = jax.ShapeDtypeStruct(low.shape, F32)
     tables = jnp.asarray(dft_parts())
     return pl.pallas_call(
         functools.partial(grad_kernel, start),
@@ -160,7 +160,7 @@
         out_specs=(VMEM, VMEM),
         scratch_shapes=[pltpu.VMEM((NS, slots, 2, PS, PS), F32)] * 2,
         compiler_params=pltpu.CompilerParams(vmem_limit_bytes=12 << 20),
-        cost_estimate=pl.CostEstimate(flops=3 * 10**9, bytes_accessed=5 * 10**6, transcendentals=0),
+        cost_estimate=pl.CostEstimate(flops=2 * 10**9, bytes_accessed=3 * 10**6, transcendentals=0),
     )(positions, counts, own, low, probe, kre, kim, diff, tables)
 
 
@@ -177,24 +177,26 @@
             out_ref[a, b, :, after] += jnp.where(lane >= s, 0.0, moved)
 
 
-def first_kernel(pos, before, up_a_ref, up_b_ref, down_ref, out_ref):
+def first_kernel(n_ups, pos, before, *refs):
+    *sources, out_ref = refs
     out_ref[...] = jnp.zeros_like(out_ref)
-    half = down_ref.shape[0]
-    for j in range(half):
-        put(out_ref, up_a_ref, j, (pos[j, 0], pos[j, 1]))
-        put(out_ref, up_b_ref, j, (pos[half + j, 0], pos[half + j, 1]))
-        put(out_ref, down_ref, j, (before[j, 0], before[j, 1]))
-
-
-def place_first(sources, positions, before, width):
-    return pl.pallas_call(
-        first_kernel,
-        in_specs=[SMEM] * 2 + [VMEM] * len(sources),
+    for parts, where in ((sources[:n_ups], pos), (sources[n_ups:], before)):
+        row = 0
+        for source in parts:
+            for j in range(source.shape[0]):
+                put(out_ref, source, j, (where[row, 0], where[row, 1]))
+                row += 1
+
+
+def place_first(ups, downs, positions, before, width):
+    return pl.pallas_call(
+        functools.partial(first_kernel, len(ups)),
+        in_specs=[SMEM] * 2 + [VMEM] * len(ups + downs),
         out_specs=VMEM,
         out_shape=jax.ShapeDtypeStruct((NS, 2, PS, width), F32),
         compiler_params=pltpu.CompilerParams(vmem_limit_bytes=12 << 20),
         cost_estimate=pl.CostEstimate(flops=10**6, bytes_accessed=7 * 10**6, transcendentals=0),
-    )(positions, before, *sources)
+    )(positions, before, *ups, *downs)
 
 
 def last_kernel(start, before, base_ref, down_ref, out_ref):
@@ -223,22 +225,18 @@
 def per_device(tile_object, probe_wave, propagator_phase, diffraction, positions, counts):
     width = tile_object.shape[3]
     slots = positions.shape[0]
-    half = slots // 2
-    before = shifted(positions, "ty", 1)
-    low_a = shifted(crop(tile_object, before, 0, half), "ty", -1)
+    groups = [(j, j + 1) for j in range(slots)]
+    own = crop(tile_object, positions, 0, slots)
+    before, own = lax.optimization_barrier((shifted(positions, "ty", 1), own))
+    lows = [shifted(crop(tile_object, before, *group), "ty", -1) for group in groups]
     kre, kim = jnp.cos(propagator_phase), jnp.sin(propagator_phase)
-    low_b = shifted(crop(tile_object, before, half, slots), "ty", -1)
-    own_a, own_b = crop(tile_object, positions, 0, half), crop(tile_object, positions, half, slots)
-
-    def pair(own, low, start):
-        return gradients(own, low, probe_wave, kre, kim, diffraction, positions, counts, start)
-
-    up_a, down_a = pair(own_a, low_a, 0)
-    down_a = shifted(down_a, "ty", 1)
-    up_b, down_b = pair(own_b, low_b, half)
-    down_b = shifted(down_b, "ty", 1)
-    base = place_first([up_a, up_b, down_a], positions, before, width)
-    return place_last(base, down_b, before, half)
+    ups, downs = [], []
+    for (start, stop), low in zip(groups, lows):
+        up, down = gradients(own, low, probe_wave, kre, kim, diffraction, positions, counts, start)
+        ups.append(up)
+        downs.append(shifted(down, "ty", 1))
+    base = place_first(ups, downs[:-1], positions, before, width)
+    return place_last(base, downs[-1], before, groups[-1][0])
 
 
 def solution(mesh):

time: 63.2 us -> 67.2 us (1.063)
  the two profiles are of different devices: /device:TPU:0 before, /device:TPU:22 now
where the time goes in v4:
time: 67.2 us; the launch traced here: 67 us
  Pallas kernels  40.2 us (60%)
  waiting for transfers between devices  15.3 us (23%)
  starting transfers between devices  7.15 us (11%)
  local copies, waits for them, and re-layouts  3.61 us (5%)
  between operations  0.78 us (1%)
    pallas_call x4, Pallas kernels, gradients(): pl.pallas_call(functools.partial(grad_kernel, start), out_shape=(out, out...  31.1 us
    ppermute x9, waiting for transfers between devices, shifted(): return lax.ppermute(x, axis, [(i, (i + by) % peers) for i in range(peers)])  15.3 us
    ppermute x9, starting transfers between devices, shifted(): return lax.ppermute(x, axis, [(i, (i + by) % peers) for i in range(peers)])  7.15 us
    pallas_call x5, Pallas kernels, crop(): pl.pallas_call(functools.partial(crop_kernel, start), in_specs=[SMEM, VME...  4.29 us
    unnamed x13, local copies, waits for them, and re-layouts  3.38 us
    pallas_call x1, Pallas kernels, place_last(): pl.pallas_call(functools.partial(last_kernel, start), grid_spec=pltpu.Pre...  2.87 us
    pallas_call x1, Pallas kernels, place_first(): pl.pallas_call(functools.partial(first_kernel, len(ups)), in_specs=[SMEM]...  1.89 us
  transfers between devices with their start and end apart: 9, of which 3 were waited for; matrix products, arithmetic and copies ran while one was open for 0% of the time, Pallas kernels for 55%

profile of v4, /device:TPU:22, one launch (start us, length us, event | category | flops | bytes accessed | tf_op | source)
XLA Modules:
  0.0 67.0 jit_solution(11478759149937028909)
XLA Ops:
  0.0 0.8 %copy.11.where.pos = s32[4,2]{1,0:T(4,128)S(1)} copy(s32[4,2]{0,1:T(2,128)} %param.14) | data formatting | bytes 64 | tf_op args[4]
  0.8 1.9 %copy-done = f32[4,2,128,768]{3,2,1,0:T(8,128)S(1)} copy-done((f32[4,2,128,768]{3,2,1,0:T(8,128)S(1)}, f32[4,2,128,768]{3,2,1,0:T(8,128)}, u32[]{:S(2)}) %copy-start) | copy-done | bytes 3145752
  2.7 1.2 %shard_map.100.own_ref = f32[4,4,2,128,128]{4,3,2,1,0:T(8,128)S(1)} custom-call(s32[4,2]{1,0:T(4,128)S(1)} %copy.11.where.pos, f32[4,2,128,768]{3,2,1,0:T(8,128)S(1)} %copy-done), custom_call_target="tpu_custom_call" | custom-call | flops 1000 | bytes 10000 | tf_op jit(solution)/shard_map/pallas_call | solution.py:53
  3.9 0.7 %copy-done.1 = f32[4,2,128,768]{3,2,1,0:T(8,128)S(1)} copy-done((f32[4,2,128,768]{3,2,1,0:T(8,128)S(1)}, f32[4,2,128,768]{3,2,1,0:T(8,128)}, u32[]{:S(2)}) %copy-start.1) | copy-done | bytes 3145752
  4.5 0.8 %shard_map.101 = f32[1,4,2,128,128]{4,3,2,1,0:T(8,128)S(1)} custom-call(s32[4,2]{1,0:T(4,128)S(1)} %collective-permute-done.where.before, f32[4,2,128,768]{3,2,1,0:T(8,128)S(1)} %copy-done.1), custom_call_target="tpu_custom_call" | custom-call | flops 1000 | bytes 10000 | tf_op jit(solution)/shard_map/pallas_call | solution.py:53
  5.3 1.8 %collective-permute-start.1 = (f32[1,4,2,128,128]{4,3,2,1,0:T(8,128)S(1)}, f32[1,4,2,128,128]{4,3,2,1,0:T(8,128)S(1)}, u32[]{:S(2)}, u32[]{:S(2)}) collective-permute-start(f32[1,4,2,128,128]{4,3,2,1,0:T(8,128)S(1)} %shard_map.101), channel_id=1, source_target_pairs={{0,15},{1,0},{2,1},{3,2},{4,3},{5,4},{6,5},{7,6},{8,7},{9,8},{10,9... | collective-permute-start | bytes 1572872 | tf_op jit(solution)/shard_map/ppermute | solution.py:21
  7.1 0.8 %shard_map.103 = f32[1,4,2,128,128]{4,3,2,1,0:T(8,128)S(1)} custom-call(s32[4,2]{1,0:T(4,128)S(1)} %collective-permute-done.where.before, f32[4,2,128,768]{3,2,1,0:T(8,128)S(1)} %copy-done.1), custom_call_target="tpu_custom_call" | custom-call | flops 1000 | bytes 10000 | tf_op jit(solution)/shard_map/pallas_call | solution.py:53
  8.7 0.8 %shard_map.105 = f32[1,4,2,128,128]{4,3,2,1,0:T(8,128)S(1)} custom-call(s32[4,2]{1,0:T(4,128)S(1)} %collective-permute-done.where.before, f32[4,2,128,768]{3,2,1,0:T(8,128)S(1)} %copy-done.1), custom_call_target="tpu_custom_call" | custom-call | flops 1000 | bytes 10000 | tf_op jit(solution)/shard_map/pallas_call | solution.py:53
  9.4 1.6 %collective-permute-start.3 = (f32[1,4,2,128,128]{4,3,2,1,0:T(8,128)S(1)}, f32[1,4,2,128,128]{4,3,2,1,0:T(8,128)S(1)}, u32[]{:S(2)}, u32[]{:S(2)}) collective-permute-start(f32[1,4,2,128,128]{4,3,2,1,0:T(8,128)S(1)} %shard_map.105), channel_id=1, source_target_pairs={{0,15},{1,0},{2,1},{3,2},{4,3},{5,4},{6,5},{7,6},{8,7},{9,8},{10,9... | collective-permute-start | bytes 1572872 | tf_op jit(solution)/shard_map/ppermute | solution.py:21
  11.0 0.2 fusion
  11.2 0.8 %shard_map.107 = f32[1,4,2,128,128]{4,3,2,1,0:T(8,128)S(1)} custom-call(s32[4,2]{1,0:T(4,128)S(1)} %collective-permute-done.where.before, f32[4,2,128,768]{3,2,1,0:T(8,128)S(1)} %copy-done.1), custom_call_target="tpu_custom_call" | custom-call | flops 1000 | bytes 10000 | tf_op jit(solution)/shard_map/pallas_call | solution.py:53
  12.0 0.1 collective-permute-start.4
  12.1 1.7 %collective-permute-done.1.low_ref = f32[1,4,2,128,128]{4,3,2,1,0:T(8,128)S(1)} collective-permute-done((f32[1,4,2,128,128]{4,3,2,1,0:T(8,128)S(1)}, f32[1,4,2,128,128]{4,3,2,1,0:T(8,128)S(1)}, u32[]{:S(2)}, u32[]{:S(2)}) %collective-permute-start.1) | collective-permute-done | bytes 524320 | tf_op jit(solution)/shard_map/ppermute | solution.py:21
  13.8 7.8 %shard_map.102 = (f32[1,4,2,128,128]{4,3,2,1,0:T(8,128)S(1)}, f32[1,4,2,128,128]{4,3,2,1,0:T(8,128)S(1)}) custom-call(s32[4,2]{1,0:T(4,128)S(1)} %copy.11.where.pos, s32[1]{0:T(128)S(6)} %copy.18.counts, f32[4,4,2,128,128]{4,3,2,1,0:T(8,128)S(1)} %shard_map.100.own_ref, f32[1,4,2,128,128]{4,3,2,1,0:T(8,128)S(1)} %collective-permute-done.1.low_ref, ...), custom_call_target="tpu_custom_call" | custom-call | flops 2000000000 | bytes 3000000 | tf_op jit(solution)/shard_map/pallas_call | solution.py:156
  21.6 2.8 %collective-permute-start.5 = (f32[1,4,2,128,128]{4,3,2,1,0:T(8,128)S(1)}, f32[1,4,2,128,128]{4,3,2,1,0:T(8,128)S(1)}, u32[]{:S(2)}, u32[]{:S(2)}) collective-permute-start(f32[1,4,2,128,128]{4,3,2,1,0:T(8,128)S(1)} %get-tuple-element.21), channel_id=1, source_target_pairs={{0,1},{1,2},{2,3},{3,4},{4,5},{5,6},{6,7},{7,8},{8,9},{9,10},{10,1... | collective-permute-start | bytes 1572872 | tf_op jit(solution)/shard_map/ppermute | solution.py:21
  24.4 7.8 %shard_map.104 = (f32[1,4,2,128,128]{4,3,2,1,0:T(8,128)S(1)}, f32[1,4,2,128,128]{4,3,2,1,0:T(8,128)S(1)}) custom-call(s32[4,2]{1,0:T(4,128)S(1)} %copy.11.where.pos, s32[1]{0:T(128)S(6)} %copy.18.counts, f32[4,4,2,128,128]{4,3,2,1,0:T(8,128)S(1)} %shard_map.100.own_ref, f32[1,4,2,128,128]{4,3,2,1,0:T(8,128)S(1)} %collective-permute-done.2.low_ref, ...), custom_call_target="tpu_custom_call" | custom-call | flops 2000000000 | bytes 3000000 | tf_op jit(solution)/shard_map/pallas_call | solution.py:156
  32.2 0.1 collective-permute-start.6
  32.3 7.8 %shard_map.106 = (f32[1,4,2,128,128]{4,3,2,1,0:T(8,128)S(1)}, f32[1,4,2,128,128]{4,3,2,1,0:T(8,128)S(1)}) custom-call(s32[4,2]{1,0:T(4,128)S(1)} %copy.11.where.pos, s32[1]{0:T(128)S(6)} %copy.18.counts, f32[4,4,2,128,128]{4,3,2,1,0:T(8,128)S(1)} %shard_map.100.own_ref, f32[1,4,2,128,128]{4,3,2,1,0:T(8,128)S(1)} %collective-permute-done.3.low_ref, ...), custom_call_target="tpu_custom_call" | custom-call | flops 2000000000 | bytes 3000000 | tf_op jit(solution)/shard_map/pallas_call | solution.py:156
  40.0 0.8 %collective-permute-start.7 = (f32[1,4,2,128,128]{4,3,2,1,0:T(8,128)S(1)}, f32[1,4,2,128,128]{4,3,2,1,0:T(8,128)S(1)}, u32[]{:S(2)}, u32[]{:S(2)}) collective-permute-start(f32[1,4,2,128,128]{4,3,2,1,0:T(8,128)S(1)} %get-tuple-element.23), channel_id=1, source_target_pairs={{0,1},{1,2},{2,3},{3,4},{4,5},{5,6},{6,7},{7,8},{8,9},{9,10},{10,1... | collective-permute-start | bytes 1572872 | tf_op jit(solution)/shard_map/ppermute | solution.py:21
  40.8 6.7 %collective-permute-done.4.low_ref = f32[1,4,2,128,128]{4,3,2,1,0:T(8,128)S(1)} collective-permute-done((f32[1,4,2,128,128]{4,3,2,1,0:T(8,128)S(1)}, f32[1,4,2,128,128]{4,3,2,1,0:T(8,128)S(1)}, u32[]{:S(2)}, u32[]{:S(2)}) %collective-permute-start.4) | collective-permute-done | bytes 524320 | tf_op jit(solution)/shard_map/ppermute | solution.py:21
  47.5 7.8 %shard_map.108 = (f32[1,4,2,128,128]{4,3,2,1,0:T(8,128)S(1)}, f32[1,4,2,128,128]{4,3,2,1,0:T(8,128)S(1)}) custom-call(s32[4,2]{1,0:T(4,128)S(1)} %copy.11.where.pos, s32[1]{0:T(128)S(6)} %copy.18.counts, f32[4,4,2,128,128]{4,3,2,1,0:T(8,128)S(1)} %shard_map.100.own_ref, f32[1,4,2,128,128]{4,3,2,1,0:T(8,128)S(1)} %collective-permute-done.4.low_ref, ...), custom_call_target="tpu_custom_call" | custom-call | flops 2000000000 | bytes 3000000 | tf_op jit(solution)/shard_map/pallas_call | solution.py:156
  55.4 1.9 %shard_map.109.base_ref = f32[4,2,128,768]{3,2,1,0:T(8,128)S(1)} custom-call(s32[4,2]{1,0:T(4,128)S(1)} %copy.11.where.pos, s32[4,2]{1,0:T(4,128)S(1)} %collective-permute-done.where.before, f32[1,4,2,128,128]{4,3,2,1,0:T(8,128)S(1)} %get-tuple-element.17.refs_0_, f32[1,4,2,128,128]{4,3,2,1,0:T(8,128)S(1)} %get-tuple-element.18.refs_1_, ...), custom_call_target="tpu_custom_call" | custom-call | flops 1000000 | bytes 7000000 | tf_op jit(solution)/shard_map/pallas_call | solution.py:192
  57.3 6.8 %collective-permute-done.8.down_ref = f32[1,4,2,128,128]{4,3,2,1,0:T(8,128)S(1)} collective-permute-done((f32[1,4,2,128,128]{4,3,2,1,0:T(8,128)S(1)}, f32[1,4,2,128,128]{4,3,2,1,0:T(8,128)S(1)}, u32[]{:S(2)}, u32[]{:S(2)}) %collective-permute-start.8) | collective-permute-done | bytes 524320 | tf_op jit(solution)/shard_map/ppermute | solution.py:21
  64.1 2.9 %shard_map.110 = f32[4,2,128,768]{3,2,1,0:T(8,128)} custom-call(s32[4,2]{1,0:T(4,128)S(1)} %collective-permute-done.where.before, f32[4,2,128,768]{3,2,1,0:T(8,128)S(1)} %shard_map.109.base_ref, f32[1,4,2,128,128]{4,3,2,1,0:T(8,128)S(1)} %collective-permute-done.8.down_ref), custom_call_target="tpu_custom_call" | custom-call | flops 1000000 | bytes 7000000 | tf_op jit(solution)/shard_map/pallas_call | solution.py:211
  (19 shorter events, 0.2 us)
Async XLA Ops:
  0.8 3.1 %collective-permute-start = (s32[4,2]{1,0:T(4,128)S(1)}, s32[4,2]{1,0:T(4,128)S(1)}, u32[]{:S(2)}, u32[]{:S(2)}) collective-permute-start(s32[4,2]{1,0:T(4,128)S(1)} %copy.11.where.pos), channel_id=1, source_target_pairs={{0,1},{1,2},{2,3},{3,4},{4,5},{5,6},{6,7},{7,8},{8,9},{9,10},{10,1... | collective-permute-start | bytes 104 | tf_op jit(solution)/shard_map/ppermute | solution.py:21
  0.8 1.9 %copy-start = (f32[4,2,128,768]{3,2,1,0:T(8,128)S(1)}, f32[4,2,128,768]{3,2,1,0:T(8,128)}, u32[]{:S(2)}) copy-start(f32[4,2,128,768]{3,2,1,0:T(8,128)} %tile_ref.9) | copy-start | bytes 9437188
  2.7 1.9 %copy-start.1 = (f32[4,2,128,768]{3,2,1,0:T(8,128)S(1)}, f32[4,2,128,768]{3,2,1,0:T(8,128)}, u32[]{:S(2)}) copy-start(f32[4,2,128,768]{3,2,1,0:T(8,128)} %tile_ref.9) | copy-start | bytes 9437188
  5.3 5.7 %copy-start.5 = (f32[128,128]{1,0:T(8,128)S(1)}, f32[128,128]{1,0:T(8,128)}, u32[]{:S(2)}) copy-start(f32[128,128]{1,0:T(8,128)} %param.12) | copy-start | bytes 196612
  5.3 8.5 %collective-permute-start.1 = (f32[1,4,2,128,128]{4,3,2,1,0:T(8,128)S(1)}, f32[1,4,2,128,128]{4,3,2,1,0:T(8,128)S(1)}, u32[]{:S(2)}, u32[]{:S(2)}) collective-permute-start(f32[1,4,2,128,128]{4,3,2,1,0:T(8,128)S(1)} %shard_map.101), channel_id=1, source_target_pairs={{0,15},{1,0},{2,1},{3,2},{4,3},{5,4},{6,5},{7,6},{8,7},{9,8},{10,9... | collective-permute-start | bytes 1572872 | tf_op jit(solution)/shard_map/ppermute | solution.py:21
  7.9 16.5 %collective-permute-start.2 = (f32[1,4,2,128,128]{4,3,2,1,0:T(8,128)S(1)}, f32[1,4,2,128,128]{4,3,2,1,0:T(8,128)S(1)}, u32[]{:S(2)}, u32[]{:S(2)}) collective-permute-start(f32[1,4,2,128,128]{4,3,2,1,0:T(8,128)S(1)} %shard_map.103), channel_id=1, source_target_pairs={{0,15},{1,0},{2,1},{3,2},{4,3},{5,4},{6,5},{7,6},{8,7},{9,8},{10,9... | collective-permute-start | bytes 1572872 | tf_op jit(solution)/shard_map/ppermute | solution.py:21
  8.6 5.2 %copy-start.2 = (f32[4,128,128]{2,1,0:T(8,128)S(1)}, f32[4,128,128]{2,1,0:T(8,128)}, u32[]{:S(2)}) copy-start(f32[4,128,128]{2,1,0:T(8,128)} %diff_ref.7) | copy-start | bytes 786436
  8.6 5.2 %copy-start.3 = (f32[2,128,128]{2,1,0:T(8,128)S(1)}, f32[2,128,128]{2,1,0:T(8,128)}, u32[]{:S(2)}) copy-start(f32[2,128,128]{2,1,0:T(8,128)} %probe_ref.7) | copy-start | bytes 393220
  8.7 5.2 %copy-start.4 = (bf16[4,256,256]{2,1,0:T(8,128)(2,1)S(1)}, bf16[4,256,256]{2,1,0:T(8,128)(2,1)}, u32[]{:S(2)}) copy-start(bf16[4,256,256]{2,1,0:T(8,128)(2,1)} %constant.2.clone.tab_ref) | copy-start | bytes 1572868
  9.4 22.8 %collective-permute-start.3 = (f32[1,4,2,128,128]{4,3,2,1,0:T(8,128)S(1)}, f32[1,4,2,128,128]{4,3,2,1,0:T(8,128)S(1)}, u32[]{:S(2)}, u32[]{:S(2)}) collective-permute-start(f32[1,4,2,128,128]{4,3,2,1,0:T(8,128)S(1)} %shard_map.105), channel_id=1, source_target_pairs={{0,15},{1,0},{2,1},{3,2},{4,3},{5,4},{6,5},{7,6},{8,7},{9,8},{10,9... | collective-permute-start | bytes 1572872 | tf_op jit(solution)/shard_map/ppermute | solution.py:21
  12.0 35.5 %collective-permute-start.4 = (f32[1,4,2,128,128]{4,3,2,1,0:T(8,128)S(1)}, f32[1,4,2,128,128]{4,3,2,1,0:T(8,128)S(1)}, u32[]{:S(2)}, u32[]{:S(2)}) collective-permute-start(f32[1,4,2,128,128]{4,3,2,1,0:T(8,128)S(1)} %shard_map.107), channel_id=1, source_target_pairs={{0,15},{1,0},{2,1},{3,2},{4,3},{5,4},{6,5},{7,6},{8,7},{9,8},{10,9... | collective-permute-start | bytes 1572872 | tf_op jit(solution)/shard_map/ppermute | solution.py:21
  21.6 33.8 %collective-permute-start.5 = (f32[1,4,2,128,128]{4,3,2,1,0:T(8,128)S(1)}, f32[1,4,2,128,128]{4,3,2,1,0:T(8,128)S(1)}, u32[]{:S(2)}, u32[]{:S(2)}) collective-permute-start(f32[1,4,2,128,128]{4,3,2,1,0:T(8,128)S(1)} %get-tuple-element.21), channel_id=1, source_target_pairs={{0,1},{1,2},{2,3},{3,4},{4,5},{5,6},{6,7},{7,8},{8,9},{9,10},{10,1... | collective-permute-start | bytes 1572872 | tf_op jit(solution)/shard_map/ppermute | solution.py:21
  32.2 23.2 %collective-permute-start.6 = (f32[1,4,2,128,128]{4,3,2,1,0:T(8,128)S(1)}, f32[1,4,2,128,128]{4,3,2,1,0:T(8,128)S(1)}, u32[]{:S(2)}, u32[]{:S(2)}) collective-permute-start(f32[1,4,2,128,128]{4,3,2,1,0:T(8,128)S(1)} %get-tuple-element.22), channel_id=1, source_target_pairs={{0,1},{1,2},{2,3},{3,4},{4,5},{5,6},{6,7},{7,8},{8,9},{9,10},{10,1... | collective-permute-start | bytes 1572872 | tf_op jit(solution)/shard_map/ppermute | solution.py:21
  40.0 15.4 %collective-permute-start.7 = (f32[1,4,2,128,128]{4,3,2,1,0:T(8,128)S(1)}, f32[1,4,2,128,128]{4,3,2,1,0:T(8,128)S(1)}, u32[]{:S(2)}, u32[]{:S(2)}) collective-permute-start(f32[1,4,2,128,128]{4,3,2,1,0:T(8,128)S(1)} %get-tuple-element.23), channel_id=1, source_target_pairs={{0,1},{1,2},{2,3},{3,4},{4,5},{5,6},{6,7},{7,8},{8,9},{9,10},{10,1... | collective-permute-start | bytes 1572872 | tf_op jit(solution)/shard_map/ppermute | solution.py:21
  55.3 8.8 %collective-permute-start.8 = (f32[1,4,2,128,128]{4,3,2,1,0:T(8,128)S(1)}, f32[1,4,2,128,128]{4,3,2,1,0:T(8,128)S(1)}, u32[]{:S(2)}, u32[]{:S(2)}) collective-permute-start(f32[1,4,2,128,128]{4,3,2,1,0:T(8,128)S(1)} %get-tuple-element.24), channel_id=1, source_target_pairs={{0,1},{1,2},{2,3},{3,4},{4,5},{5,6},{6,7},{7,8},{8,9},{9,10},{10,1... | collective-permute-start | bytes 1572872 | tf_op jit(solution)/shard_map/ppermute | solution.py:21
